TPU v7x, 32 devices: a whole 2x2x4 slice. The times are simulated.
32 devices in a mesh: leaf: 16 (over z, y, x), rhs: 2 (over core).
Axes of the slice: x: 2, y: 2, z: 4, core: 2. Of those that a mesh axis runs over, the one named last changes fastest.
Arguments:
- rhs_block: float32 [16384, 2048], P(('leaf', 'rhs')), may hold values from -6 to 6
- leaf_inverse: float32 [16384, 1024], P('leaf', 'rhs'), may hold values from -0.1875 to 0.1875
- leaf_basis: float32 [16384, 128], P('leaf'), may hold values from -0.1875 to 0.1875
- couple_one: float32 [2048, 512], P('leaf'), may hold values from -0.25 to 0.25
- basis_one: float32 [2048, 128], P('leaf'), may hold values from -0.25 to 0.25
- couple_two: float32 [512, 512], P('leaf'), may hold values from -0.25 to 0.25
- basis_two: float32 [512, 128], P('leaf'), may hold values from -0.25 to 0.25
- root_inverse: float32 [128, 128], P('leaf'), may hold values from -0.5 to 0.5
- leaf_slot: int32 [16], replicated, may hold values from 0 to 3, as said below
- node_slot: int32 [4], replicated, may hold values from 0 to 3, as said below
Outputs:
- solution: float32 [16384, 2048], P('leaf', 'rhs')
Inputs may be any that keep to these rules, and one draw needn't show every extreme that they name: `leaf_slot`: in every aligned group of four leaves the four entries are a permutation of 0 to 3. `node_slot`: in every aligned group of four first-level nodes the four entries are a permutation of 0 to 3.
All inputs are finite; a program needn't handle non-finite values.
Results may differ from a plain program's by a relative error of at most 0.00007.
Values sent between devices are 32-bit elements; how exact they have to be, the bound alone decides.
No kernel may reach another device: no remote copies, remote signals or barrier semaphores. Data moves between devices by JAX's collectives and lax.ppermute only.
A program may use at most 128 MiB of HBM per device.

v0:
```python
import functools

import jax
import jax.numpy as jnp
from jax import lax
from jax.experimental import pallas as pl
from jax.experimental.pallas import tpu as pltpu
from jax.sharding import PartitionSpec as P


F32 = jnp.float32
BF16 = jnp.bfloat16


def split(value):
    high = value.astype(BF16)
    return high, (value - high.astype(F32)).astype(BF16)


def dot(left, right):
    return jnp.dot(left, right, preferred_element_type=F32)


def dot_parts(left_high, left_low, right_high, right_low):
    rows = left_high.shape[0]
    both = dot(jnp.concatenate([left_high, left_low], 0), right_high)
    return both[:rows] + both[rows:] + dot(left_high, right_low)


def dot_split(left, right):
    return dot_parts(*split(left), *split(right))


def call(body, out_shapes, scalars, operands, flops, limit_mib=16, scratch=()):
    moved = sum(o.size * o.dtype.itemsize for o in list(operands) + list(out_shapes))
    vmem = pl.BlockSpec(memory_space=pltpu.VMEM)
    return pl.pallas_call(
        body,
        out_shape=out_shapes,
        in_specs=[pl.BlockSpec(memory_space=pltpu.SMEM)] * len(scalars) + [vmem] * len(operands),
        out_specs=[vmem] * len(out_shapes),
        scratch_shapes=scratch,
        compiler_params=pltpu.CompilerParams(vmem_limit_bytes=limit_mib << 20),
        cost_estimate=pl.CostEstimate(flops=flops, bytes_accessed=moved, transcendentals=0),
    )(*scalars, *operands)


def struct(*shape, dtype=F32):
    return jax.ShapeDtypeStruct(shape, dtype)


def coeff_body(
    arity, ids, basis, inverse, rhs, couple_one, basis_one, couple_two, basis_two, root,
    send, own, inverse_high, inverse_low, other_high, other_low, own_high, own_low, joined, packed, mixed,
    basis_here, inverse_here, rhs_here, turned, projected, sems,
):
    member, core = ids[0] % arity, ids[1]
    rank, half = send.shape
    width = half // arity
    couple = couple_one.shape[1]
    share = couple_two.shape[0]
    root_rows, wide = root.shape
    piece = min(wide, couple)
    chunk = basis.shape[0] // arity
    count = iter(range(sems.shape[0]))

    def fetch(source, target):
        copy = pltpu.make_async_copy(source, target, sems.at[next(count)])
        copy.start()
        return copy

    basis_copy = fetch(basis, basis_here)
    inverse_copies = [
        fetch(inverse.at[step * chunk : (step + 1) * chunk], inverse_here.at[step * chunk : (step + 1) * chunk])
        for step in range(arity)
    ]
    rhs_copies = []
    for side in range(2):
        for bits in range(arity):
            column = (((1 - core) if side == 0 else core) * arity + (member ^ bits)) * width
            at = (side * arity + bits) * width
            rhs_copies.append(
                fetch(rhs.at[:, pl.ds(pl.multiple_of(column, width), width)], rhs_here.at[:, at : at + width])
            )
            if side == 0 and bits == arity - 1:
                matrix_copies = [
                    fetch(couple_one, joined.at[:, :couple]),
                    fetch(basis_one, joined.at[:, couple:]),
                    fetch(couple_two, packed.at[:share, :couple]),
                    fetch(basis_two, packed.at[:share, couple:]),
                ]
                for part in range(wide // piece):
                    low = share + part * root_rows
                    matrix_copies.append(
                        fetch(
                            root.at[:, part * piece : (part + 1) * piece],
                            packed.at[low : low + root_rows, :piece],
                        )
                    )

    packed[share:, piece:] = jnp.zeros_like(packed[share:, piece:])
    basis_copy.wait()
    high, low = split(basis_here[...].T)
    turned[:rank] = high
    turned[rank:] = low
    both = first = 0.0
    for step in range(arity):
        rows = slice(step * chunk, (step + 1) * chunk)
        inverse_copies[step].wait()
        high, low = split(inverse_here[rows])
        inverse_high[rows] = high
        inverse_low[rows] = low
        both = both + dot(turned[:, rows], high)
        first = first + dot(turned[:rank, rows], low)
    high, low = split(both[:rank] + both[rank:] + first)
    projected[:rank] = high
    projected[rank:] = low
    for side, (out, out_high, out_low) in enumerate(((send, other_high, other_low), (own, own_high, own_low))):
        for bits in range(arity):
            at = (side * arity + bits) * width
            columns = slice(bits * width, (bits + 1) * width)
            rhs_copies[side * arity + bits].wait()
            high, low = split(rhs_here[:, at : at + width])
            out_high[:, columns] = high
            out_low[:, columns] = low
            both = dot(projected[...], high)
            out[:, columns] = both[:rank] + both[rank:] + dot(projected[:rank], low)
    for copy in matrix_copies:
        copy.wait()

    @pl.when(core == 0)
    def _():
        mixed[...] = joined[...]

    @pl.when(core != 0)
    def _():
        mixed[: packed.shape[0]] = packed[...]
        mixed[packed.shape[0] :] = jnp.zeros_like(mixed[packed.shape[0] :])


def leaf_body(add, inverse_high, inverse_low, rhs_high, rhs_low, *rest):
    out = rest[-1]
    tile = out.shape[0] // 4

    @pl.loop(0, 4)
    def _(step):
        rows = pl.ds(pl.multiple_of(step * tile, tile), tile)
        left_high, left_low = inverse_high[rows], inverse_low[rows]
        value = dot(left_high, rhs_high[...]) + dot(left_high, rhs_low[...]) + dot(left_low, rhs_high[...])
        out[rows] = value + rest[0][rows] if add else value


def leaf_product(inverse, rhs, extra=()):
    rows, depth = inverse[0].shape
    half = rhs[0].shape[1]
    return call(
        functools.partial(leaf_body, len(extra) > 0),
        [struct(rows, half)],
        [],
        [*inverse, *rhs, *extra],
        6 * rows * depth * half,
    )[0]


def pieces_body(own, got, *outs):
    width = outs[0].shape[1]
    for bits, out in enumerate(outs):
        columns = slice(bits * width, (bits + 1) * width)
        out[...] = own[:, columns] + got[:, columns]


def first_body(arity, ids, mine, near, near_other, mixed, mixed_other, joined, reduced):
    member, core = ids[0] % arity, ids[1]
    couple = reduced.shape[1]
    joined[member] = mine[...]
    joined[member ^ (1 + core)] = near[...]
    joined[member ^ (2 - core)] = near_other[...]

    @pl.when(core == 0)
    def _():
        joined[member ^ 3] = mixed[...]

    @pl.when(core != 0)
    def _():
        joined[member ^ 3] = mixed_other[...]

    everything = joined[...].reshape(-1, joined.shape[-1])
    reduced[...] = dot_split(everything[:, couple:].T, everything[:, :couple])


def column_body(arity, share, root_rows, wide, ids, packed, mixed, mixed_other, rest, rest_other, column, part):
    node, core = ids[0] // arity, ids[1]
    place = node % arity
    rank = column.shape[1] - wide_couple(share, arity)
    couple = column.shape[1] - rank
    piece = min(wide, couple)
    units = wide // piece
    lanes = couple // piece

    def put(distance, ref):
        index = place ^ distance
        column[pl.ds(pl.multiple_of(index * share, share), share)] = ref[:share]
        for unit in range(units):
            number = index * units + unit
            strip, lane = number // lanes, number % lanes
            column[
                pl.ds(pl.multiple_of(arity * share + strip * root_rows, root_rows), root_rows),
                pl.ds(pl.multiple_of(lane * piece, piece), piece),
            ] = ref[share + unit * root_rows : share + (unit + 1) * root_rows, :piece]

    column[arity * share :] = jnp.zeros_like(column[arity * share :])
    put(0, packed)

    @pl.when(core == 0)
    def _():
        put(1, mixed_other)
        put(2, rest)
        put(3, rest_other)

    @pl.when(core != 0)
    def _():
        put(1, mixed)
        put(2, rest_other)
        put(3, rest)

    height = part.shape[0]
    part[...] = column[pl.ds(pl.multiple_of(core * height, 8), height)]


def wide_couple(share, arity):
    return share * arity * arity


def node_up_body(arity, ids, slots, reduced, *refs):
    pieces, (coeff, stack) = refs[:arity], refs[arity:]
    member, node = ids[0] % arity, ids[0] // arity
    rank = pieces[0].shape[0]
    for bits in range(arity):
        place = slots[node * arity + (member ^ bits)]
        stack[pl.ds(pl.multiple_of(place * rank, rank), rank)] = pieces[bits][...]
    coeff[...] = dot_split(reduced[...], stack[...])


def node_solve_body(arity, ids, slots, joined, stack, solve, basis):
    member, node = ids[0] % arity, ids[0] // arity
    couple = stack.shape[0]
    rank = joined.shape[1]
    high, low = split(stack[...])
    blocks = []
    for bits in range(arity):
        place = slots[node * arity + (member ^ bits)]
        block = joined[place]
        basis[bits * rank : (bits + 1) * rank] = block[:, couple:]
        blocks.append(block[:, :couple])
    left_high, left_low = split(jnp.concatenate(blocks, 0))
    solve[...] = dot(left_high, high) + dot(left_high, low) + dot(left_low, high)


def second_body(arity, share, root_rows, wide, ids, node_slots, mine, near, near_other, far, far_other, *refs):
    outs, everything, root_all = refs[:-2], refs[-2], refs[-1]
    member, core = ids[0] % arity, ids[1]
    node = ids[0] // arity
    couple = wide_couple(share, arity)
    rank = everything.shape[1] - couple
    piece = min(wide, couple)
    units = wide // piece
    lanes = couple // piece

    def put(distance, pieces):
        def rows(start, count):
            ref = pieces[start // pieces[0].shape[0]]
            start = start % pieces[0].shape[0]
            return ref[start : start + count]

        for place in range(arity):
            index = place * arity + (member ^ distance)
            for low in range(0, share, 8):
                everything[pl.ds(pl.multiple_of(index * share + low, 8), 8)] = rows(place * share + low, 8)
            for unit in range(units):
                number = place * units + unit
                strip, lane = number // lanes, number % lanes
                root_all[
                    pl.ds(pl.multiple_of(index * root_rows, root_rows), root_rows),
                    unit * piece : (unit + 1) * piece,
                ] = rows(arity * share + strip * root_rows, root_rows)[:, lane * piece : (lane + 1) * piece]

    put(0, [mine])

    @pl.when(core == 0)
    def _():
        put(1, [near])
        put(2, [near_other])
        put(3, [far, far_other])

    @pl.when(core != 0)
    def _():
        put(1, [near_other])
        put(2, [near])
        put(3, [far_other, far])

    matrices = everything[...]
    reduced = dot_split(matrices[:, couple:].T, matrices[:, :couple])
    rows = everything[pl.ds(pl.multiple_of(node_slots[node] * rank, rank), rank)]
    if len(outs) == 1:
        root_coeff = dot_split(root_all[...], reduced)
        outs[0][...] = rows[:, :couple] - dot_split(rows[:, couple:], root_coeff)
    else:
        outs[0][...] = rows
        outs[1][...] = reduced
        outs[2][...] = root_all[...]


def place_second(arity, ids, node_slots, uppers, stack):
    node = ids[0] // arity
    rank = uppers[0].shape[0]
    for bits in range(arity):
        place = node_slots[node ^ bits]
        stack[pl.ds(pl.multiple_of(place * rank, rank), rank)] = uppers[bits][...]


def down_body(arity, ids, node_slots, down_map, solve, basis, *refs):
    uppers, outs, stack = refs[:arity], refs[arity:-1], refs[-1]
    place_second(arity, ids, node_slots, uppers, stack)
    upper_down = dot_split(down_map[...], stack[...])
    down = solve[...] - dot_split(basis[...], upper_down)
    rank = outs[0].shape[0]
    for bits in range(arity):
        outs[bits][...] = down[bits * rank : (bits + 1) * rank]


def stack_second_body(arity, ids, node_slots, *refs):
    place_second(arity, ids, node_slots, refs[:arity], refs[arity])


def subtract_body(arity, ids, upper_down, solve, basis, *outs):
    down = solve[...] - dot_split(basis[...], upper_down[...])
    rank = outs[0].shape[0]
    for bits in range(arity):
        outs[bits][...] = down[bits * rank : (bits + 1) * rank]


def final_body(arity, ids, base, basis, *refs):
    pieces, (out, left, high, low) = refs[:arity], refs[arity:]
    step = pl.program_id(0)
    rank = pieces[0].shape[0]

    @pl.when(step == 0)
    def _():
        left_high, left_low = split(basis[...])
        left[:, :rank] = left_high
        left[:, rank:] = left_low
        for bits in range(arity):
            piece_high, piece_low = split(pieces[bits][...])
            high[bits, :rank] = piece_high
            high[bits, rank:] = piece_high
            low[bits] = piece_low

    width = out.shape[1]
    columns = pl.ds(pl.multiple_of(step * width, width), width)
    out[...] = base[:, columns] - (dot(left[...], high[step]) + dot(left[:, :rank], low[step]))


def swap(block, bits):
    count = lax.axis_size("leaf")
    return lax.ppermute(block, "leaf", [(low, low ^ bits) for low in range(count)])


def swap_core(block):
    return lax.ppermute(block, "rhs", [(0, 1), (1, 0)])


def swap_each(block, bits):
    count = lax.axis_size("leaf")
    route = [
        (2 * low + core, 2 * (low ^ bits[core]) + core)
        for low in range(count)
        for core in range(2)
        if bits[core] is not None
    ]
    return lax.ppermute(block, ("leaf", "rhs"), route)


def per_device(
    rhs_block,
    leaf_inverse,
    leaf_basis,
    couple_one,
    basis_one,
    couple_two,
    basis_two,
    root_inverse,
    leaf_slot,
    node_slot,
):
    position = lax.axis_index("leaf")
    devices = lax.axis_size("leaf")
    core = lax.axis_index("rhs")
    points, rank = leaf_basis.shape
    couple = couple_one.shape[1]
    arity = couple // rank
    group = arity * arity
    tops = devices // group
    depth = rhs_block.shape[0]
    half = rhs_block.shape[1] // lax.axis_size("rhs")
    width = half // arity
    share = couple_two.shape[0]
    root_rows, wide = root_inverse.shape
    joined_width = couple + rank
    packed_rows = share + root_rows * (wide // min(wide, couple))
    ids = jnp.stack([position, core]).astype(jnp.int32)

    vmem = pl.BlockSpec(memory_space=pltpu.VMEM)
    large = [leaf_basis, leaf_inverse, rhs_block, couple_one, basis_one, couple_two, basis_two, root_inverse]
    coeff = pl.pallas_call(
        functools.partial(coeff_body, arity),
        out_shape=[struct(rank, half)] * 2
        + [struct(points, depth, dtype=BF16)] * 2
        + [struct(depth, half, dtype=BF16)] * 4
        + [struct(rank, joined_width), struct(packed_rows, joined_width), struct(rank, joined_width)],
        in_specs=[pl.BlockSpec(memory_space=pltpu.SMEM)] + [pl.BlockSpec(memory_space=pl.ANY)] * len(large),
        out_specs=[vmem] * 11,
        scratch_shapes=[
            pltpu.VMEM((points, rank), F32),
            pltpu.VMEM((points, depth), F32),
            pltpu.VMEM((depth, 2 * half), F32),
            pltpu.VMEM((2 * rank, points), BF16),
            pltpu.VMEM((2 * rank, depth), BF16),
            pltpu.SemaphoreType.DMA((5 + 3 * arity + wide // min(wide, couple),)),
        ],
        compiler_params=pltpu.CompilerParams(vmem_limit_bytes=16 << 20),
        cost_estimate=pl.CostEstimate(
            flops=6 * rank * depth * (points + 2 * half), bytes_accessed=14 << 20, transcendentals=0
        ),
    )
    coeff_send, coeff_own, *halves, joined_mine, packed, mixed_mine = coeff(
        ids, *[pltpu.with_memory_space_constraint(array, pltpu.HBM) for array in large]
    )
    inverse_parts, rhs_other, rhs_own = halves[:2], halves[2:4], halves[4:]
    coeff_got = swap_core(coeff_send)

    near = swap_each(joined_mine, (1, 2))
    mixed = swap_each(mixed_mine, (3, arity))
    rest = swap_each(packed, (2 * arity, 3 * arity))

    near_other = swap_core(near)
    mixed_other = swap_core(mixed)
    rest_other = swap_core(rest)
    joined, reduced_one = call(
        functools.partial(first_body, arity),
        [struct(arity, rank, joined_width), struct(rank, couple)],
        [ids],
        [joined_mine, near, near_other, mixed, mixed_other],
        6 * couple * rank * couple,
    )

    column_rows = arity * share + root_rows * (arity * wide // couple)
    column_half = -(-column_rows // 16) * 8
    column, column_part = call(
        functools.partial(column_body, arity, share, root_rows, wide),
        [struct(2 * column_half, joined_width), struct(column_half, joined_width)],
        [ids],
        [packed, mixed, mixed_other, rest, rest_other],
        0,
    )
    column_near = swap_each(column, (1, 2))
    column_far = swap(column_part, 3)
    column_near_other = swap_core(column_near)
    column_far_other = swap_core(column_far)

    pieces = call(pieces_body, [struct(rank, width)] * arity, [], [coeff_own, coeff_got], rank * half)
    pieces = [pieces[0]] + [swap(pieces[bits], bits) for bits in range(1, arity)]
    node_coeff, stack_one = call(
        functools.partial(node_up_body, arity),
        [struct(rank, width), struct(couple, width)],
        [ids, leaf_slot],
        [reduced_one, *pieces],
        6 * rank * couple * width,
    )
    uppers = [node_coeff] + [swap(node_coeff, arity * bits) for bits in range(1, arity)]
    node_solve, basis_rows = call(
        functools.partial(node_solve_body, arity),
        [struct(couple, width), struct(couple, rank)],
        [ids, leaf_slot],
        [joined, stack_one],
        6 * couple * couple * width,
    )

    if tops == 1:
        outs = [struct(rank, couple)]
    else:
        outs = [struct(rank, joined_width), struct(rank, couple), struct(rank, wide)]
    second = call(
        functools.partial(second_body, arity, share, root_rows, wide),
        outs,
        [ids, node_slot],
        [column, column_near, column_near_other, column_far, column_far_other],
        6 * couple * rank * couple,
        scratch=[pltpu.VMEM((couple, joined_width), F32), pltpu.VMEM((rank, wide), F32)],
    )
    if tops == 1:
        back = call(
            functools.partial(down_body, arity),
            [struct(rank, width)] * arity,
            [ids, node_slot],
            [second[0], node_solve, basis_rows, *uppers],
            12 * rank * couple * width,
            scratch=[pltpu.VMEM((couple, width), F32)],
        )
    else:
        mul = functools.partial(jnp.dot, precision=lax.Precision.HIGHEST)
        rows, reduced_two, root_all = second
        stack_two = call(
            functools.partial(stack_second_body, arity),
            [struct(couple, width)],
            [ids, node_slot],
            uppers,
            couple * width,
        )[0]
        upper_coeff = mul(reduced_two, stack_two)
        tops_coeff = jnp.stack([upper_coeff] + [swap(upper_coeff, group * bits) for bits in range(1, tops)])
        order = jnp.arange(tops, dtype=jnp.int32) ^ (position // group)
        tops_coeff = jnp.take(tops_coeff, order, axis=0).reshape(tops * rank, width)
        root_solve = mul(root_all, tops_coeff)
        upper_down = mul(rows[:, :couple], stack_two) - mul(rows[:, couple:], root_solve)
        back = call(
            functools.partial(subtract_body, arity),
            [struct(rank, width)] * arity,
            [ids],
            [upper_down, node_solve, basis_rows],
            6 * rank * couple * width,
        )
    back = [back[0]] + [swap(back[bits], bits) for bits in range(1, arity)]

    solve_got = swap_core(leaf_product(inverse_parts, rhs_other))
    base = leaf_product(inverse_parts, rhs_own, [solve_got])
    return pl.pallas_call(
        functools.partial(final_body, arity),
        out_shape=struct(points, half),
        grid_spec=pltpu.PrefetchScalarGridSpec(
            num_scalar_prefetch=1,
            grid=(arity,),
            in_specs=[vmem] * (2 + arity),
            out_specs=pl.BlockSpec((points, width), lambda i, ids: (0, (ids[0] % arity) ^ i)),
            scratch_shapes=[
                pltpu.VMEM((points, 2 * rank), BF16),
                pltpu.VMEM((arity, 2 * rank, width), BF16),
                pltpu.VMEM((arity, rank, width), BF16),
            ],
        ),
        compiler_params=pltpu.CompilerParams(vmem_limit_bytes=16 << 20),
        cost_estimate=pl.CostEstimate(
            flops=6 * points * rank * half, bytes_accessed=8 * points * half, transcendentals=0
        ),
    )(ids, base, leaf_basis, *back)


def solution(mesh):
    return jax.shard_map(
        per_device,
        mesh=mesh,
        in_specs=(
            P(("leaf", "rhs"), None),
            P("leaf", "rhs"),
            P("leaf", None),
            P("leaf", None),
            P("leaf", None),
            P("leaf", None),
            P("leaf", None),
            P("leaf", None),
            P(),
            P(),
        ),
        out_specs=P("leaf", "rhs"),
        check_vma=False,
    )
```

profile of v0, /device:TPU:0, one launch (start us, length us, event | category | flops | bytes accessed | tf_op | source)
XLA Modules:
  0.0 81.1 jit_solution(16607172167419950687)
XLA Ops:
  0.0 0.1 pad_add_fusion.ids
  0.1 5.9 %shard_map.100 = (f32[128,1024]{1,0:T(8,128)S(1)}, f32[128,1024]{1,0:T(8,128)S(1)}, bf16[1024,512]{1,0:T(8,128)(2,1)S(1)}, bf16[1024,512]{1,0:T(8,128)(2,1)S(1)}...) custom-call(s32[2]{0:T(128)S(1)} %pad_add_fusion.ids, ...), custom_call_target="tpu_custom_call" | custom-call | flops 1207959552 | bytes 14680064 | tf_op jit(solution)/shard_map/pallas_call | solution.py:435
  6.0 0.0 copy-start.1
  6.0 3.9 %shard_map.101 = f32[1024,1024]{1,0:T(8,128)S(1)} custom-call(bf16[1024,512]{1,0:T(8,128)(2,1)S(1)} %get-tuple-element.32.inverse_high, bf16[1024,512]{1,0:T(8,128)(2,1)S(1)} %get-tuple-element.33.inverse_low, bf16[512,1024]{1,0:T(8,128)(2,1)S(1)} %get-tuple-element.36.rhs_high, bf16[512,1024]{1,0:T(8,128)(2,1)S(1)} %get-tuple-element.37.rhs_low), custom_call_target="tpu_custom_call" | custom-call | flops 3221225472 | bytes 8388608 | tf_op jit(solution)/shard_map/pallas_call | solution.py:37
  9.9 0.0 copy-start.2
  9.9 0.5 collective-permute-start
  10.5 3.5 %collective-permute-start.1 = (f32[128,640]{1,0:T(8,128)S(1)}, f32[128,640]{1,0:T(8,128)S(1)}, u32[]{:S(2)}, u32[]{:S(2)}) collective-permute-start(f32[128,640]{1,0:T(8,128)S(1)} %get-tuple-element.39), channel_id=1, source_target_pairs={{0,6},{1,9},{2,4},{3,11},{4,2},{5,13},{6,0},{7,15},{8,14},{9,1},{1... | collective-permute-start | bytes 983048 | tf_op jit(solution)/shard_map/ppermute | solution.py:380
  14.0 5.1 %collective-permute-done.1.mixed = f32[128,640]{1,0:T(8,128)S(1)} collective-permute-done((f32[128,640]{1,0:T(8,128)S(1)}, f32[128,640]{1,0:T(8,128)S(1)}, u32[]{:S(2)}, u32[]{:S(2)}) %collective-permute-start.1) | collective-permute-done | bytes 327712 | tf_op jit(solution)/shard_map/ppermute | solution.py:380
  19.0 0.0 collective-permute-start.2
  19.1 3.1 %collective-permute-start.3 = (f32[40,640]{1,0:T(8,128)S(1)}, f32[40,640]{1,0:T(8,128)S(1)}, u32[]{:S(2)}, u32[]{:S(2)}) collective-permute-start(f32[40,640]{1,0:T(8,128)S(1)} %get-tuple-element.38.packed), channel_id=1, source_target_pairs={{0,16},{1,25},{2,18},{3,27},{4,20},{5,29},{6,22},{7,31},{8,24},{9,... | collective-permute-start | bytes 307208 | tf_op jit(solution)/shard_map/ppermute | solution.py:380
  22.1 1.2 %collective-permute-start.11 = (f32[128,1024]{1,0:T(8,128)S(1)}, f32[128,1024]{1,0:T(8,128)S(1)}, u32[]{:S(2)}, u32[]{:S(2)}) collective-permute-start(f32[128,1024]{1,0:T(8,128)S(1)} %get-tuple-element.46), channel_id=1, source_target_pairs={{0,1},{1,0},{2,3},{3,2},{4,5},{5,4},{6,7},{7,6},{8,9},{9,8},{10,11... | collective-permute-start | bytes 1572872 | tf_op jit(solution)/shard_map/ppermute | solution.py:369
  23.3 1.5 %collective-permute-start.9 = (f32[128,640]{1,0:T(8,128)S(1)}, f32[128,640]{1,0:T(8,128)S(1)}, u32[]{:S(2)}, u32[]{:S(2)}) collective-permute-start(f32[128,640]{1,0:T(8,128)S(1)} %get-tuple-element.42.mine), channel_id=1, source_target_pairs={{0,2},{1,5},{2,0},{3,7},{4,6},{5,1},{6,4},{7,3},{8,10},{9,13},{10,... | collective-permute-start | bytes 983048 | tf_op jit(solution)/shard_map/ppermute | solution.py:380
  24.8 3.2 %collective-permute-done.3.rest = f32[40,640]{1,0:T(8,128)S(1)} collective-permute-done((f32[40,640]{1,0:T(8,128)S(1)}, f32[40,640]{1,0:T(8,128)S(1)}, u32[]{:S(2)}, u32[]{:S(2)}) %collective-permute-start.3) | collective-permute-done | bytes 102432 | tf_op jit(solution)/shard_map/ppermute | solution.py:380
  28.0 0.0 collective-permute-start.4
  28.0 1.3 %collective-permute-done.4.rest_other = f32[40,640]{1,0:T(8,128)S(1)} collective-permute-done((f32[40,640]{1,0:T(8,128)S(1)}, f32[40,640]{1,0:T(8,128)S(1)}, u32[]{:S(2)}, u32[]{:S(2)}) %collective-permute-start.4) | collective-permute-done | bytes 102432 | tf_op jit(solution)/shard_map/ppermute | solution.py:369
  29.3 0.0 collective-permute-done.2.mixed_other
  29.3 0.6 shard_map.103
  30.0 1.6 %collective-permute-start.5 = (f32[144,640]{1,0:T(8,128)S(1)}, f32[144,640]{1,0:T(8,128)S(1)}, u32[]{:S(2)}, u32[]{:S(2)}) collective-permute-start(f32[144,640]{1,0:T(8,128)S(1)} %get-tuple-element.40.mine), channel_id=1, source_target_pairs={{0,2},{1,5},{2,0},{3,7},{4,6},{5,1},{6,4},{7,3},{8,10},{9,13},{10,... | collective-permute-start | bytes 1105928 | tf_op jit(solution)/shard_map/ppermute | solution.py:380
  31.5 0.0 collective-permute-done.9.near
  31.5 0.0 collective-permute-start.10
  31.5 1.5 %collective-permute-start.7 = (f32[72,640]{1,0:T(8,128)S(1)}, f32[72,640]{1,0:T(8,128)S(1)}, u32[]{:S(2)}, u32[]{:S(2)}) collective-permute-start(f32[72,640]{1,0:T(8,128)S(1)} %get-tuple-element.41), channel_id=1, source_target_pairs={{0,6},{2,4},{4,2},{6,0},{8,14},{10,12},{12,10},{14,8},{16,22},{18,... | collective-permute-start | bytes 552968 | tf_op jit(solution)/shard_map/ppermute | solution.py:365
  33.0 0.0 collective-permute-done.11.got
  33.0 0.1 shard_map.106
  33.1 1.6 %collective-permute-start.12 = (f32[128,256]{1,0:T(8,128)S(1)}, f32[128,256]{1,0:T(8,128)S(1)}, u32[]{:S(2)}, u32[]{:S(2)}) collective-permute-start(f32[128,256]{1,0:T(8,128)S(1)} %get-tuple-element.48), channel_id=1, source_target_pairs={{0,2},{2,0},{4,6},{6,4},{8,10},{10,8},{12,14},{14,12},{16,18},{18,... | collective-permute-start | bytes 393224 | tf_op jit(solution)/shard_map/ppermute | solution.py:365
  34.6 4.9 %collective-permute-done.5.near = f32[144,640]{1,0:T(8,128)S(1)} collective-permute-done((f32[144,640]{1,0:T(8,128)S(1)}, f32[144,640]{1,0:T(8,128)S(1)}, u32[]{:S(2)}, u32[]{:S(2)}) %collective-permute-start.5) | collective-permute-done | bytes 368672 | tf_op jit(solution)/shard_map/ppermute | solution.py:380
  39.5 0.0 collective-permute-start.6
  39.5 4.3 %collective-permute-done.7.far = f32[72,640]{1,0:T(8,128)S(1)} collective-permute-done((f32[72,640]{1,0:T(8,128)S(1)}, f32[72,640]{1,0:T(8,128)S(1)}, u32[]{:S(2)}, u32[]{:S(2)}) %collective-permute-start.7) | collective-permute-done | bytes 184352 | tf_op jit(solution)/shard_map/ppermute | solution.py:365
  43.9 0.0 collective-permute-start.8
  43.9 0.0 collective-permute-done.10.near_other
  43.9 0.5 collective-permute-start.13
  44.4 0.0 collective-permute-done.12.refs_1_
  44.4 2.4 %collective-permute-start.14 = (f32[128,256]{1,0:T(8,128)S(1)}, f32[128,256]{1,0:T(8,128)S(1)}, u32[]{:S(2)}, u32[]{:S(2)}) collective-permute-start(f32[128,256]{1,0:T(8,128)S(1)} %get-tuple-element.50), channel_id=1, source_target_pairs={{0,6},{2,4},{4,2},{6,0},{8,14},{10,12},{12,10},{14,8},{16,22},{18,... | collective-permute-start | bytes 393224 | tf_op jit(solution)/shard_map/ppermute | solution.py:365
  46.8 1.1 %shard_map.105 = (f32[4,128,640]{2,1,0:T(8,128)S(1)}, f32[128,512]{1,0:T(8,128)S(1)}) custom-call(s32[2]{0:T(128)S(1)} %pad_add_fusion.ids, f32[128,640]{1,0:T(8,128)S(1)} %get-tuple-element.42.mine, f32[128,640]{1,0:T(8,128)S(1)} %collective-permute-done.9.near, f32[128,640]{1,0:T(8,128)S(1)} %collective-permute-done.10.near_other, ...), custom_call_target="tpu_custom_call" | custom-call | flops 201326592 | bytes 3211264 | tf_op jit(solution)/shard_map/pallas_call | solution.py:37
  47.9 4.7 %collective-permute-done.13.refs_2_ = f32[128,256]{1,0:T(8,128)S(1)} collective-permute-done((f32[128,256]{1,0:T(8,128)S(1)}, f32[128,256]{1,0:T(8,128)S(1)}, u32[]{:S(2)}, u32[]{:S(2)}) %collective-permute-start.13) | collective-permute-done | bytes 131104 | tf_op jit(solution)/shard_map/ppermute | solution.py:365
  52.6 0.0 collective-permute-done.14.refs_3_
  52.6 0.0 copy-done.1
  52.6 0.9 %shard_map.107 = (f32[128,256]{1,0:T(8,128)S(1)}, f32[512,256]{1,0:T(8,128)S(1)}) custom-call(s32[2]{0:T(128)S(1)} %pad_add_fusion.ids, s32[16]{0:T(128)S(1)} %copy-done.1, f32[128,512]{1,0:T(8,128)S(1)} %get-tuple-element.44.reduced, f32[128,256]{1,0:T(8,128)S(1)} %get-tuple-element.47.refs_0_, f32[128,256]{1,0:T(8,128)S(1)} %collective-permute-done.12.refs_1_, ...), custom_call_target="tpu_custom_call" | custom-call | flops 100663296 | bytes 1441792 | tf_op jit(solution)/shard_map/pallas_call | solution.py:37
  53.5 2.8 %collective-permute-start.17 = (f32[128,256]{1,0:T(8,128)S(1)}, f32[128,256]{1,0:T(8,128)S(1)}, u32[]{:S(2)}, u32[]{:S(2)}) collective-permute-start(f32[128,256]{1,0:T(8,128)S(1)} %get-tuple-element.54.refs_0_), channel_id=1, source_target_pairs={{0,24},{2,26},{4,28},{6,30},{8,16},{10,18},{12,20},{14,22},{16,8},... | collective-permute-start | bytes 393224 | tf_op jit(solution)/shard_map/ppermute | solution.py:365
  56.3 0.0 collective-permute-start.16
  56.3 0.0 collective-permute-done.8.far_other
  56.3 1.6 %collective-permute-start.15 = (f32[128,256]{1,0:T(8,128)S(1)}, f32[128,256]{1,0:T(8,128)S(1)}, u32[]{:S(2)}, u32[]{:S(2)}) collective-permute-start(f32[128,256]{1,0:T(8,128)S(1)} %get-tuple-element.54.refs_0_), channel_id=1, source_target_pairs={{0,8},{2,10},{4,12},{6,14},{8,0},{10,2},{12,4},{14,6},{16,24},{18,... | collective-permute-start | bytes 393224 | tf_op jit(solution)/shard_map/ppermute | solution.py:365
  57.9 1.1 %shard_map.108 = (f32[512,256]{1,0:T(8,128)S(1)}, f32[512,128]{1,0:T(8,128)S(1)}) custom-call(s32[2]{0:T(128)S(1)} %pad_add_fusion.ids, s32[16]{0:T(128)S(1)} %copy-done.1, f32[4,128,640]{2,1,0:T(8,128)S(1)} %get-tuple-element.43.joined, f32[512,256]{1,0:T(8,128)S(1)} %get-tuple-element.51.stack), custom_call_target="tpu_custom_call" | custom-call | flops 402653184 | bytes 2621440 | tf_op jit(solution)/shard_map/pallas_call | solution.py:37
  59.1 0.0 collective-permute-done.6.near_other
  59.1 0.0 copy-done.2
  59.1 1.6 %shard_map.104.down_map = f32[128,512]{1,0:T(8,128)S(1)} custom-call(s32[2]{0:T(128)S(1)} %pad_add_fusion.ids, s32[4]{0:T(128)S(1)} %copy-done.2, f32[144,640]{1,0:T(8,128)S(1)} %get-tuple-element.40.mine, f32[144,640]{1,0:T(8,128)S(1)} %collective-permute-done.5.near, f32[144,640]{1,0:T(8,128)S(1)} %collective-permute-done.6.near_other, ...), custom_call_target="tpu_custom_call" | custom-call | flops 201326592 | bytes 1736704 | tf_op jit(solution)/shard_map/pallas_call | solution.py:37
  60.7 1.1 %collective-permute-done.17.refs_3_ = f32[128,256]{1,0:T(8,128)S(1)} collective-permute-done((f32[128,256]{1,0:T(8,128)S(1)}, f32[128,256]{1,0:T(8,128)S(1)}, u32[]{:S(2)}, u32[]{:S(2)}) %collective-permute-start.17) | collective-permute-done | bytes 131104 | tf_op jit(solution)/shard_map/ppermute | solution.py:365
  61.8 4.7 %collective-permute-done.16.refs_2_ = f32[128,256]{1,0:T(8,128)S(1)} collective-permute-done((f32[128,256]{1,0:T(8,128)S(1)}, f32[128,256]{1,0:T(8,128)S(1)}, u32[]{:S(2)}, u32[]{:S(2)}) %collective-permute-start.16) | collective-permute-done | bytes 131104 | tf_op jit(solution)/shard_map/ppermute | solution.py:365
  66.4 0.0 collective-permute-done.15.refs_1_
  66.4 1.4 %shard_map.109 = (f32[128,256]{1,0:T(8,128)S(1)}, f32[128,256]{1,0:T(8,128)S(1)}, f32[128,256]{1,0:T(8,128)S(1)}, f32[128,256]{1,0:T(8,128)S(1)}) custom-call(s32[2]{0:T(128)S(1)} %pad_add_fusion.ids, s32[4]{0:T(128)S(1)} %copy-done.2, f32[128,512]{1,0:T(8,128)S(1)} %shard_map.104.down_map, f32[512,256]{1,0:T(8,128)S(1)} %get-tuple-element.52.solve, ...), custom_call_target="tpu_custom_call" | custom-call | flops 201326592 | bytes 2097152 | tf_op jit(solution)/shard_map/pallas_call | solution.py:37
  67.8 1.6 %collective-permute-start.18 = (f32[128,256]{1,0:T(8,128)S(1)}, f32[128,256]{1,0:T(8,128)S(1)}, u32[]{:S(2)}, u32[]{:S(2)}) collective-permute-start(f32[128,256]{1,0:T(8,128)S(1)} %get-tuple-element.56), channel_id=1, source_target_pairs={{0,2},{2,0},{4,6},{6,4},{8,10},{10,8},{12,14},{14,12},{16,18},{18,... | collective-permute-start | bytes 393224 | tf_op jit(solution)/shard_map/ppermute | solution.py:365
  69.4 0.5 collective-permute-start.19
  69.9 1.5 %collective-permute-start.20 = (f32[128,256]{1,0:T(8,128)S(1)}, f32[128,256]{1,0:T(8,128)S(1)}, u32[]{:S(2)}, u32[]{:S(2)}) collective-permute-start(f32[128,256]{1,0:T(8,128)S(1)} %get-tuple-element.58), channel_id=1, source_target_pairs={{0,6},{2,4},{4,2},{6,0},{8,14},{10,12},{12,10},{14,8},{16,22},{18,... | collective-permute-start | bytes 393224 | tf_op jit(solution)/shard_map/ppermute | solution.py:365
  71.4 0.0 collective-permute-done.rest_0_
  71.4 0.0 copy-start
  71.4 3.9 %shard_map.102.base = f32[1024,1024]{1,0:T(8,128)S(1)} custom-call(bf16[1024,512]{1,0:T(8,128)(2,1)S(1)} %get-tuple-element.32.inverse_high, bf16[1024,512]{1,0:T(8,128)(2,1)S(1)} %get-tuple-element.33.inverse_low, bf16[512,1024]{1,0:T(8,128)(2,1)S(1)} %get-tuple-element.34.rhs_high, bf16[512,1024]{1,0:T(8,128)(2,1)S(1)} %get-tuple-element.35.rhs_low, ...), custom_call_target="tpu_custom_call" | custom-call | flops 3221225472 | bytes 12582912 | tf_op jit(solution)/shard_map/pallas_call | solution.py:37
  75.3 0.0 collective-permute-done.18.refs_1_
  75.3 1.8 %collective-permute-done.19.refs_2_ = f32[128,256]{1,0:T(8,128)S(1)} collective-permute-done((f32[128,256]{1,0:T(8,128)S(1)}, f32[128,256]{1,0:T(8,128)S(1)}, u32[]{:S(2)}, u32[]{:S(2)}) %collective-permute-start.19) | collective-permute-done | bytes 131104 | tf_op jit(solution)/shard_map/ppermute | solution.py:365
  77.1 0.0 collective-permute-done.20.refs_3_
  77.1 0.0 copy-done
  77.1 4.0 %shard_map.110 = f32[1024,1024]{1,0:T(8,128)} custom-call(s32[2]{0:T(128)S(1)} %pad_add_fusion.ids, f32[1024,1024]{1,0:T(8,128)S(1)} %shard_map.102.base, f32[1024,128]{1,0:T(8,128)S(1)} %copy-done, f32[128,256]{1,0:T(8,128)S(1)} %get-tuple-element.55.refs_0_, f32[128,256]{1,0:T(8,128)S(1)} %collective-permute-done.18.refs_1_, ...), custom_call_target="tpu_custom_call" | custom-call | flops 805306368 | bytes 8388608 | tf_op jit(solution)/shard_map/pallas_call | solution.py:536
Async XLA Ops:
  6.0 46.6 %copy-start.1 = (s32[16]{0:T(128)S(1)}, s32[16]{0:T(128)}, u32[]{:S(2)}) copy-start(s32[16]{0:T(128)} %slots.3) | copy-start | bytes 196
  9.9 49.2 %copy-start.2 = (s32[4]{0:T(128)S(1)}, s32[4]{0:T(128)}, u32[]{:S(2)}) copy-start(s32[4]{0:T(128)} %node_slots.3) | copy-start | bytes 52
  9.9 61.5 %collective-permute-start = (f32[1024,1024]{1,0:T(8,128)S(1)}, f32[1024,1024]{1,0:T(8,128)S(1)}, u32[]{:S(2)}, u32[]{:S(2)}) collective-permute-start(f32[1024,1024]{1,0:T(8,128)S(1)} %shard_map.101), channel_id=1, source_target_pairs={{0,1},{1,0},{2,3},{3,2},{4,5},{5,4},{6,7},{7,6},{8,9},{9,8},{10,11... | collective-permute-start | bytes 12582920 | tf_op jit(solution)/shard_map/ppermute | solution.py:369
  10.5 8.6 %collective-permute-start.1 = (f32[128,640]{1,0:T(8,128)S(1)}, f32[128,640]{1,0:T(8,128)S(1)}, u32[]{:S(2)}, u32[]{:S(2)}) collective-permute-start(f32[128,640]{1,0:T(8,128)S(1)} %get-tuple-element.39), channel_id=1, source_target_pairs={{0,6},{1,9},{2,4},{3,11},{4,2},{5,13},{6,0},{7,15},{8,14},{9,1},{1... | collective-permute-start | bytes 983048 | tf_op jit(solution)/shard_map/ppermute | solution.py:380
  19.0 10.3 %collective-permute-start.2 = (f32[128,640]{1,0:T(8,128)S(1)}, f32[128,640]{1,0:T(8,128)S(1)}, u32[]{:S(2)}, u32[]{:S(2)}) collective-permute-start(f32[128,640]{1,0:T(8,128)S(1)} %collective-permute-done.1.mixed), channel_id=1, source_target_pairs={{0,1},{1,0},{2,3},{3,2},{4,5},{5,4},{6,7},{7,6},{8,9},{9,8},{10,11... | collective-permute-start | bytes 983048 | tf_op jit(solution)/shard_map/ppermute | solution.py:369
  19.1 9.0 %collective-permute-start.3 = (f32[40,640]{1,0:T(8,128)S(1)}, f32[40,640]{1,0:T(8,128)S(1)}, u32[]{:S(2)}, u32[]{:S(2)}) collective-permute-start(f32[40,640]{1,0:T(8,128)S(1)} %get-tuple-element.38.packed), channel_id=1, source_target_pairs={{0,16},{1,25},{2,18},{3,27},{4,20},{5,29},{6,22},{7,31},{8,24},{9,... | collective-permute-start | bytes 307208 | tf_op jit(solution)/shard_map/ppermute | solution.py:380
  22.1 10.9 %collective-permute-start.11 = (f32[128,1024]{1,0:T(8,128)S(1)}, f32[128,1024]{1,0:T(8,128)S(1)}, u32[]{:S(2)}, u32[]{:S(2)}) collective-permute-start(f32[128,1024]{1,0:T(8,128)S(1)} %get-tuple-element.46), channel_id=1, source_target_pairs={{0,1},{1,0},{2,3},{3,2},{4,5},{5,4},{6,7},{7,6},{8,9},{9,8},{10,11... | collective-permute-start | bytes 1572872 | tf_op jit(solution)/shard_map/ppermute | solution.py:369
  23.3 8.2 %collective-permute-start.9 = (f32[128,640]{1,0:T(8,128)S(1)}, f32[128,640]{1,0:T(8,128)S(1)}, u32[]{:S(2)}, u32[]{:S(2)}) collective-permute-start(f32[128,640]{1,0:T(8,128)S(1)} %get-tuple-element.42.mine), channel_id=1, source_target_pairs={{0,2},{1,5},{2,0},{3,7},{4,6},{5,1},{6,4},{7,3},{8,10},{9,13},{10,... | collective-permute-start | bytes 983048 | tf_op jit(solution)/shard_map/ppermute | solution.py:380
  28.0 1.3 %collective-permute-start.4 = (f32[40,640]{1,0:T(8,128)S(1)}, f32[40,640]{1,0:T(8,128)S(1)}, u32[]{:S(2)}, u32[]{:S(2)}) collective-permute-start(f32[40,640]{1,0:T(8,128)S(1)} %collective-permute-done.3.rest), channel_id=1, source_target_pairs={{0,1},{1,0},{2,3},{3,2},{4,5},{5,4},{6,7},{7,6},{8,9},{9,8},{10,11... | collective-permute-start | bytes 307208 | tf_op jit(solution)/shard_map/ppermute | solution.py:369
  30.0 9.5 %collective-permute-start.5 = (f32[144,640]{1,0:T(8,128)S(1)}, f32[144,640]{1,0:T(8,128)S(1)}, u32[]{:S(2)}, u32[]{:S(2)}) collective-permute-start(f32[144,640]{1,0:T(8,128)S(1)} %get-tuple-element.40.mine), channel_id=1, source_target_pairs={{0,2},{1,5},{2,0},{3,7},{4,6},{5,1},{6,4},{7,3},{8,10},{9,13},{10,... | collective-permute-start | bytes 1105928 | tf_op jit(solution)/shard_map/ppermute | solution.py:380
  31.5 12.3 %collective-permute-start.10 = (f32[128,640]{1,0:T(8,128)S(1)}, f32[128,640]{1,0:T(8,128)S(1)}, u32[]{:S(2)}, u32[]{:S(2)}) collective-permute-start(f32[128,640]{1,0:T(8,128)S(1)} %collective-permute-done.9.near), channel_id=1, source_target_pairs={{0,1},{1,0},{2,3},{3,2},{4,5},{5,4},{6,7},{7,6},{8,9},{9,8},{10,11... | collective-permute-start | bytes 983048 | tf_op jit(solution)/shard_map/ppermute | solution.py:369
  31.5 12.3 %collective-permute-start.7 = (f32[72,640]{1,0:T(8,128)S(1)}, f32[72,640]{1,0:T(8,128)S(1)}, u32[]{:S(2)}, u32[]{:S(2)}) collective-permute-start(f32[72,640]{1,0:T(8,128)S(1)} %get-tuple-element.41), channel_id=1, source_target_pairs={{0,6},{2,4},{4,2},{6,0},{8,14},{10,12},{12,10},{14,8},{16,22},{18,... | collective-permute-start | bytes 552968 | tf_op jit(solution)/shard_map/ppermute | solution.py:365
  33.1 11.3 %collective-permute-start.12 = (f32[128,256]{1,0:T(8,128)S(1)}, f32[128,256]{1,0:T(8,128)S(1)}, u32[]{:S(2)}, u32[]{:S(2)}) collective-permute-start(f32[128,256]{1,0:T(8,128)S(1)} %get-tuple-element.48), channel_id=1, source_target_pairs={{0,2},{2,0},{4,6},{6,4},{8,10},{10,8},{12,14},{14,12},{16,18},{18,... | collective-permute-start | bytes 393224 | tf_op jit(solution)/shard_map/ppermute | solution.py:365
  39.5 19.6 %collective-permute-start.6 = (f32[144,640]{1,0:T(8,128)S(1)}, f32[144,640]{1,0:T(8,128)S(1)}, u32[]{:S(2)}, u32[]{:S(2)}) collective-permute-start(f32[144,640]{1,0:T(8,128)S(1)} %collective-permute-done.5.near), channel_id=1, source_target_pairs={{0,1},{1,0},{2,3},{3,2},{4,5},{5,4},{6,7},{7,6},{8,9},{9,8},{10,11... | collective-permute-start | bytes 1105928 | tf_op jit(solution)/shard_map/ppermute | solution.py:369
  43.9 12.4 %collective-permute-start.8 = (f32[72,640]{1,0:T(8,128)S(1)}, f32[72,640]{1,0:T(8,128)S(1)}, u32[]{:S(2)}, u32[]{:S(2)}) collective-permute-start(f32[72,640]{1,0:T(8,128)S(1)} %collective-permute-done.7.far), channel_id=1, source_target_pairs={{0,1},{1,0},{2,3},{3,2},{4,5},{5,4},{6,7},{7,6},{8,9},{9,8},{10,11... | collective-permute-start | bytes 552968 | tf_op jit(solution)/shard_map/ppermute | solution.py:369
  43.9 8.7 %collective-permute-start.13 = (f32[128,256]{1,0:T(8,128)S(1)}, f32[128,256]{1,0:T(8,128)S(1)}, u32[]{:S(2)}, u32[]{:S(2)}) collective-permute-start(f32[128,256]{1,0:T(8,128)S(1)} %get-tuple-element.49), channel_id=1, source_target_pairs={{0,4},{2,6},{4,0},{6,2},{8,12},{10,14},{12,8},{14,10},{16,20},{18,... | collective-permute-start | bytes 393224 | tf_op jit(solution)/shard_map/ppermute | solution.py:365
  44.4 8.2 %collective-permute-start.14 = (f32[128,256]{1,0:T(8,128)S(1)}, f32[128,256]{1,0:T(8,128)S(1)}, u32[]{:S(2)}, u32[]{:S(2)}) collective-permute-start(f32[128,256]{1,0:T(8,128)S(1)} %get-tuple-element.50), channel_id=1, source_target_pairs={{0,6},{2,4},{4,2},{6,0},{8,14},{10,12},{12,10},{14,8},{16,22},{18,... | collective-permute-start | bytes 393224 | tf_op jit(solution)/shard_map/ppermute | solution.py:365
  53.5 8.3 %collective-permute-start.17 = (f32[128,256]{1,0:T(8,128)S(1)}, f32[128,256]{1,0:T(8,128)S(1)}, u32[]{:S(2)}, u32[]{:S(2)}) collective-permute-start(f32[128,256]{1,0:T(8,128)S(1)} %get-tuple-element.54.refs_0_), channel_id=1, source_target_pairs={{0,24},{2,26},{4,28},{6,30},{8,16},{10,18},{12,20},{14,22},{16,8},... | collective-permute-start | bytes 393224 | tf_op jit(solution)/shard_map/ppermute | solution.py:365
  56.3 10.1 %collective-permute-start.16 = (f32[128,256]{1,0:T(8,128)S(1)}, f32[128,256]{1,0:T(8,128)S(1)}, u32[]{:S(2)}, u32[]{:S(2)}) collective-permute-start(f32[128,256]{1,0:T(8,128)S(1)} %get-tuple-element.54.refs_0_), channel_id=1, source_target_pairs={{0,16},{2,18},{4,20},{6,22},{8,24},{10,26},{12,28},{14,30},{16,0},... | collective-permute-start | bytes 393224 | tf_op jit(solution)/shard_map/ppermute | solution.py:365
  56.3 10.1 %collective-permute-start.15 = (f32[128,256]{1,0:T(8,128)S(1)}, f32[128,256]{1,0:T(8,128)S(1)}, u32[]{:S(2)}, u32[]{:S(2)}) collective-permute-start(f32[128,256]{1,0:T(8,128)S(1)} %get-tuple-element.54.refs_0_), channel_id=1, source_target_pairs={{0,8},{2,10},{4,12},{6,14},{8,0},{10,2},{12,4},{14,6},{16,24},{18,... | collective-permute-start | bytes 393224 | tf_op jit(solution)/shard_map/ppermute | solution.py:365
  67.8 7.5 %collective-permute-start.18 = (f32[128,256]{1,0:T(8,128)S(1)}, f32[128,256]{1,0:T(8,128)S(1)}, u32[]{:S(2)}, u32[]{:S(2)}) collective-permute-start(f32[128,256]{1,0:T(8,128)S(1)} %get-tuple-element.56), channel_id=1, source_target_pairs={{0,2},{2,0},{4,6},{6,4},{8,10},{10,8},{12,14},{14,12},{16,18},{18,... | collective-permute-start | bytes 393224 | tf_op jit(solution)/shard_map/ppermute | solution.py:365
  69.4 7.7 %collective-permute-start.19 = (f32[128,256]{1,0:T(8,128)S(1)}, f32[128,256]{1,0:T(8,128)S(1)}, u32[]{:S(2)}, u32[]{:S(2)}) collective-permute-start(f32[128,256]{1,0:T(8,128)S(1)} %get-tuple-element.57), channel_id=1, source_target_pairs={{0,4},{2,6},{4,0},{6,2},{8,12},{10,14},{12,8},{14,10},{16,20},{18,... | collective-permute-start | bytes 393224 | tf_op jit(solution)/shard_map/ppermute | solution.py:365
  69.9 7.2 %collective-permute-start.20 = (f32[128,256]{1,0:T(8,128)S(1)}, f32[128,256]{1,0:T(8,128)S(1)}, u32[]{:S(2)}, u32[]{:S(2)}) collective-permute-start(f32[128,256]{1,0:T(8,128)S(1)} %get-tuple-element.58), channel_id=1, source_target_pairs={{0,6},{2,4},{4,2},{6,0},{8,14},{10,12},{12,10},{14,8},{16,22},{18,... | collective-permute-start | bytes 393224 | tf_op jit(solution)/shard_map/ppermute | solution.py:365
  71.4 5.7 %copy-start = (f32[1024,128]{1,0:T(8,128)S(1)}, f32[1024,128]{1,0:T(8,128)}, u32[]{:S(2)}) copy-start(f32[1024,128]{1,0:T(8,128)} %basis.3) | copy-start | bytes 1572868
where the time goes:
time: 81.2 us; the launch traced here: 81.1 us
  waiting for transfers between devices  31 us (38%)
  starting transfers between devices  25.4 us (31%)
  Pallas kernels  24.5 us (30%)
    ppermute x10, waiting for transfers between devices, swap(): lax.ppermute(block, 'leaf', [(low, low ^ bits) for low in range(count)])  16.6 us
    pallas_call x9, Pallas kernels, call(): pl.pallas_call(body, out_shape=out_shapes, in_specs=[pl.BlockSpec(memory_...  14.6 us
    ppermute x10, starting transfers between devices, swap(): lax.ppermute(block, 'leaf', [(low, low ^ bits) for low in range(count)])  14 us
    ppermute x4, waiting for transfers between devices, swap_each(): return lax.ppermute(block, ('leaf', 'rhs'), route)  13.1 us
    ppermute x4, starting transfers between devices, swap_each(): return lax.ppermute(block, ('leaf', 'rhs'), route)  9.64 us
    pallas_call x1, Pallas kernels, per_device(): coeff(ids, *[pltpu.with_memory_space_constraint(array, pltpu.HBM) for arr...  5.91 us
    pallas_call x1, Pallas kernels, per_device(): pl.pallas_call(functools.partial(final_body, arity), out_shape=struct(poi...  3.98 us
    ppermute x7, starting transfers between devices, swap_core(): return lax.ppermute(block, 'rhs', [(0, 1), (1, 0)])  1.78 us
  transfers between devices with their start and end apart: 21, of which 9 were waited for; matrix products, arithmetic and copies ran while one was open for 0% of the time, Pallas kernels for 13%

commit v1 on v0

--- a/solution.py
+++ b/solution.py
@@ -51,7 +51,7 @@
 
 def coeff_body(
     arity, ids, basis, inverse, rhs, couple_one, basis_one, couple_two, basis_two, root,
-    send, own, inverse_high, inverse_low, other_high, other_low, own_high, own_low, joined, packed, mixed,
+    send, own, basis_parts, inverse_high, inverse_low, other_high, other_low, own_high, own_low, joined, packed, mixed,
     basis_here, inverse_here, rhs_here, turned, projected, sems,
 ):
     member, core = ids[0] % arity, ids[1]
@@ -99,32 +99,69 @@
                     )
 
     packed[share:, piece:] = jnp.zeros_like(packed[share:, piece:])
+
+    def parts(source, rows, columns, out_high, out_low, out_columns):
+        for low_row in range(rows.start, rows.stop, 64):
+            at = slice(low_row, low_row + 64)
+            high, low = split(source[at, columns])
+            out_high[at, out_columns] = high
+            out_low[at, out_columns] = low
+
     basis_copy.wait()
-    high, low = split(basis_here[...].T)
-    turned[:rank] = high
-    turned[rank:] = low
-    both = first = 0.0
+    points = basis.shape[0]
+    for low_row in range(0, points, rank):
+        at = slice(low_row, low_row + rank)
+        value = basis_here[at]
+        high, low = split(value)
+        basis_parts[at, :rank] = high
+        basis_parts[at, rank : 2 * rank] = low
+        basis_parts[at, 2 * rank :] = high
+        high, low = split(value.T)
+        turned[:rank, at] = high
+        turned[rank:, at] = low
     for step in range(arity):
-        rows = slice(step * chunk, (step + 1) * chunk)
         inverse_copies[step].wait()
-        high, low = split(inverse_here[rows])
-        inverse_high[rows] = high
-        inverse_low[rows] = low
-        both = both + dot(turned[:, rows], high)
-        first = first + dot(turned[:rank, rows], low)
-    high, low = split(both[:rank] + both[rank:] + first)
-    projected[:rank] = high
-    projected[rank:] = low
-    for side, (out, out_high, out_low) in enumerate(((send, other_high, other_low), (own, own_high, own_low))):
-        for bits in range(arity):
-            at = (side * arity + bits) * width
-            columns = slice(bits * width, (bits + 1) * width)
-            rhs_copies[side * arity + bits].wait()
-            high, low = split(rhs_here[:, at : at + width])
-            out_high[:, columns] = high
-            out_low[:, columns] = low
-            both = dot(projected[...], high)
-            out[:, columns] = both[:rank] + both[rank:] + dot(projected[:rank], low)
+        everything = slice(0, inverse.shape[1])
+        parts(
+            inverse_here, slice(step * chunk, (step + 1) * chunk), everything, inverse_high, inverse_low, everything
+        )
+    depth = inverse.shape[1]
+    blocks = [
+        (side, bits, out, out_high, out_low)
+        for side, (out, out_high, out_low) in enumerate(((send, other_high, other_low), (own, own_high, own_low)))
+        for bits in range(arity)
+    ]
+
+    def prepare(number):
+        side, bits, _, out_high, out_low = blocks[number]
+        at = (side * arity + bits) * width
+        columns = slice(bits * width, (bits + 1) * width)
+        parts(rhs_here, slice(0, depth), slice(at, at + width), out_high, out_low, columns)
+
+    def multiply(number):
+        _, bits, out, out_high, out_low = blocks[number]
+        columns = slice(bits * width, (bits + 1) * width)
+        both = dot(projected[...], out_high[:, columns])
+        out[:, columns] = both[:rank] + both[rank:] + dot(projected[:rank], out_low[:, columns])
+
+    for number in range(2):
+        rhs_copies[number].wait()
+    for low_column in range(0, depth, width):
+        columns = slice(low_column, low_column + width)
+        both = dot(turned[...], inverse_high[:, columns])
+        high, low = split(both[:rank] + both[rank:] + dot(turned[:rank], inverse_low[:, columns]))
+        projected[:rank, columns] = high
+        projected[rank:, columns] = low
+    prepare(0)
+    prepare(1)
+    for number in range(0, len(blocks), 2):
+        later = range(number + 2, min(number + 4, len(blocks)))
+        for other in later:
+            rhs_copies[other].wait()
+        multiply(number)
+        multiply(number + 1)
+        for other in later:
+            prepare(other)
     for copy in matrix_copies:
         copy.wait()
 
@@ -169,26 +206,31 @@
         out[...] = own[:, columns] + got[:, columns]
 
 
-def first_body(arity, ids, mine, near, near_other, mixed, mixed_other, joined, reduced):
+def first_body(arity, ids, mine, one, one_other, two, two_other, joined, reduced):
     member, core = ids[0] % arity, ids[1]
-    couple = reduced.shape[1]
+    couple = reduced.shape[1] // 3
     joined[member] = mine[...]
-    joined[member ^ (1 + core)] = near[...]
-    joined[member ^ (2 - core)] = near_other[...]
 
     @pl.when(core == 0)
     def _():
-        joined[member ^ 3] = mixed[...]
+        joined[member ^ 1] = one[...]
+        joined[member ^ 2] = two[...]
+        joined[member ^ 3] = two_other[...]
 
     @pl.when(core != 0)
     def _():
-        joined[member ^ 3] = mixed_other[...]
+        joined[member ^ 1] = one_other[...]
+        joined[member ^ 2] = two_other[...]
+        joined[member ^ 3] = two[...]
 
     everything = joined[...].reshape(-1, joined.shape[-1])
-    reduced[...] = dot_split(everything[:, couple:].T, everything[:, :couple])
-
-
-def column_body(arity, share, root_rows, wide, ids, packed, mixed, mixed_other, rest, rest_other, column, part):
+    high, low = split(dot_split(everything[:, couple:].T, everything[:, :couple]))
+    reduced[:, :couple] = high
+    reduced[:, couple : 2 * couple] = low
+    reduced[:, 2 * couple :] = high
+
+
+def column_body(arity, share, root_rows, wide, ids, packed, one, one_other, three, three_other, column, part):
     node, core = ids[0] // arity, ids[1]
     place = node % arity
     rank = column.shape[1] - wide_couple(share, arity)
@@ -213,15 +255,15 @@
 
     @pl.when(core == 0)
     def _():
-        put(1, mixed_other)
-        put(2, rest)
-        put(3, rest_other)
+        put(1, one_other)
+        put(2, three)
+        put(3, three_other)
 
     @pl.when(core != 0)
     def _():
-        put(1, mixed)
-        put(2, rest_other)
-        put(3, rest)
+        put(1, one)
+        put(2, three_other)
+        put(3, three)
 
     height = part.shape[0]
     part[...] = column[pl.ds(pl.multiple_of(core * height, 8), height)]
@@ -235,17 +277,19 @@
     pieces, (coeff, stack) = refs[:arity], refs[arity:]
     member, node = ids[0] % arity, ids[0] // arity
     rank = pieces[0].shape[0]
+    couple = arity * rank
     for bits in range(arity):
         place = slots[node * arity + (member ^ bits)]
-        stack[pl.ds(pl.multiple_of(place * rank, rank), rank)] = pieces[bits][...]
-    coeff[...] = dot_split(reduced[...], stack[...])
+        high, low = split(pieces[bits][...])
+        for part, value in enumerate((high, high, low)):
+            stack[pl.ds(pl.multiple_of(part * couple + place * rank, rank), rank)] = value
+    coeff[...] = dot(reduced[...], stack[...])
 
 
 def node_solve_body(arity, ids, slots, joined, stack, solve, basis):
     member, node = ids[0] % arity, ids[0] // arity
-    couple = stack.shape[0]
+    couple = stack.shape[0] // 3
     rank = joined.shape[1]
-    high, low = split(stack[...])
     blocks = []
     for bits in range(arity):
         place = slots[node * arity + (member ^ bits)]
@@ -253,10 +297,10 @@
         basis[bits * rank : (bits + 1) * rank] = block[:, couple:]
         blocks.append(block[:, :couple])
     left_high, left_low = split(jnp.concatenate(blocks, 0))
-    solve[...] = dot(left_high, high) + dot(left_high, low) + dot(left_low, high)
-
-
-def second_body(arity, share, root_rows, wide, ids, node_slots, mine, near, near_other, far, far_other, *refs):
+    solve[...] = dot(jnp.concatenate([left_high, left_low, left_high], 1), stack[...])
+
+
+def second_body(arity, share, root_rows, wide, ids, node_slots, mine, near, near_other, far, far_other, basis_rows, *refs):
     outs, everything, root_all = refs[:-2], refs[-2], refs[-1]
     member, core = ids[0] % arity, ids[1]
     node = ids[0] // arity
@@ -303,33 +347,41 @@
     rows = everything[pl.ds(pl.multiple_of(node_slots[node] * rank, rank), rank)]
     if len(outs) == 1:
         root_coeff = dot_split(root_all[...], reduced)
-        outs[0][...] = rows[:, :couple] - dot_split(rows[:, couple:], root_coeff)
+        down_map = rows[:, :couple] - dot_split(rows[:, couple:], root_coeff)
+        left_high, left_low = split(basis_rows[...])
+        high, low = split(down_map)
+        high, low = split(dot(left_high, high) + dot(left_high, low) + dot(left_low, high))
+        outs[0][:, :couple] = high
+        outs[0][:, couple : 2 * couple] = low
+        outs[0][:, 2 * couple :] = high
     else:
         outs[0][...] = rows
         outs[1][...] = reduced
         outs[2][...] = root_all[...]
 
 
-def place_second(arity, ids, node_slots, uppers, stack):
-    node = ids[0] // arity
-    rank = uppers[0].shape[0]
+def second_rows(arity, ids, node_slots, bits, rank):
+    place = node_slots[ids[0] // arity ^ bits]
+    return pl.ds(pl.multiple_of(place * rank, rank), rank)
+
+
+def down_body(arity, ids, node_slots, down_map, solve, *refs):
+    uppers, outs, stack = refs[:arity], refs[arity:-1], refs[-1]
+    rank = outs[0].shape[0]
+    couple = arity * rank
     for bits in range(arity):
-        place = node_slots[node ^ bits]
-        stack[pl.ds(pl.multiple_of(place * rank, rank), rank)] = uppers[bits][...]
-
-
-def down_body(arity, ids, node_slots, down_map, solve, basis, *refs):
-    uppers, outs, stack = refs[:arity], refs[arity:-1], refs[-1]
-    place_second(arity, ids, node_slots, uppers, stack)
-    upper_down = dot_split(down_map[...], stack[...])
-    down = solve[...] - dot_split(basis[...], upper_down)
-    rank = outs[0].shape[0]
+        place = node_slots[ids[0] // arity ^ bits]
+        high, low = split(uppers[bits][...])
+        for part, value in enumerate((high, high, low)):
+            stack[pl.ds(pl.multiple_of(part * couple + place * rank, rank), rank)] = value
     for bits in range(arity):
-        outs[bits][...] = down[bits * rank : (bits + 1) * rank]
+        rows = slice(bits * rank, (bits + 1) * rank)
+        outs[bits][...] = solve[rows] - dot(down_map[rows], stack[...])
 
 
 def stack_second_body(arity, ids, node_slots, *refs):
-    place_second(arity, ids, node_slots, refs[:arity], refs[arity])
+    for bits in range(arity):
+        refs[arity][second_rows(arity, ids, node_slots, bits, refs[0].shape[0])] = refs[bits][...]
 
 
 def subtract_body(arity, ids, upper_down, solve, basis, *outs):
@@ -339,25 +391,57 @@
         outs[bits][...] = down[bits * rank : (bits + 1) * rank]
 
 
-def final_body(arity, ids, base, basis, *refs):
-    pieces, (out, left, high, low) = refs[:arity], refs[arity:]
-    step = pl.program_id(0)
-    rank = pieces[0].shape[0]
-
-    @pl.when(step == 0)
-    def _():
-        left_high, left_low = split(basis[...])
-        left[:, :rank] = left_high
-        left[:, rank:] = left_low
-        for bits in range(arity):
-            piece_high, piece_low = split(pieces[bits][...])
-            high[bits, :rank] = piece_high
-            high[bits, rank:] = piece_high
-            low[bits] = piece_low
-
-    width = out.shape[1]
-    columns = pl.ds(pl.multiple_of(step * width, width), width)
-    out[...] = base[:, columns] - (dot(left[...], high[step]) + dot(left[:, :rank], low[step]))
+def final_body(first, arity, ids, base, left, *refs):
+    here, right, sems = refs[-3:]
+    out = refs[-4]
+    pieces = [ref for ref in refs[:-4] if 3 * ref.shape[0] == left.shape[1]]
+    member = ids[0] % arity
+    rank, width = pieces[0].shape
+    parts = sems.shape[1]
+    tall = here.shape[0] // parts
+    copies = []
+    for number, piece in enumerate(pieces):
+        columns = slice(number * width, (number + 1) * width)
+        source = slice((number + first) * width, (number + first + 1) * width)
+        high, low = split(piece[...])
+        right[:rank, columns] = high
+        right[rank : 2 * rank, columns] = high
+        right[2 * rank :, columns] = low
+        target = pl.ds(pl.multiple_of((member ^ (number + first)) * width, width), width)
+        for part in range(parts):
+            rows = slice(part * tall, (part + 1) * tall)
+            here[rows, columns] = base[rows, source] - dot(left[rows], right[:, columns])
+            copy = pltpu.make_async_copy(here.at[rows, columns], out.at[rows, target], sems.at[number, part])
+            copy.start()
+            copies.append(copy)
+    for copy in copies:
+        copy.wait()
+
+
+def final(ids, base, left, first, pieces, so_far=None):
+    rank, width = pieces[0].shape
+    points, half = base.shape
+    vmem = pl.BlockSpec(memory_space=pltpu.VMEM)
+    hbm = pl.BlockSpec(memory_space=pltpu.HBM)
+    more = [] if so_far is None else [so_far]
+    return pl.pallas_call(
+        functools.partial(final_body, first, half // width),
+        out_shape=struct(points, half),
+        in_specs=[pl.BlockSpec(memory_space=pltpu.SMEM)] + [vmem] * (2 + len(pieces)) + [hbm] * len(more),
+        out_specs=hbm,
+        scratch_shapes=[
+            pltpu.VMEM((points, len(pieces) * width), F32),
+            pltpu.VMEM((3 * rank, len(pieces) * width), BF16),
+            pltpu.SemaphoreType.DMA((len(pieces), 4)),
+        ],
+        input_output_aliases={3 + len(pieces): 0} if more else {},
+        compiler_params=pltpu.CompilerParams(vmem_limit_bytes=16 << 20),
+        cost_estimate=pl.CostEstimate(
+            flops=6 * points * rank * width * len(pieces),
+            bytes_accessed=8 * points * width * len(pieces),
+            transcendentals=0,
+        ),
+    )(ids, base, left, *pieces, *more)
 
 
 def swap(block, bits):
@@ -414,11 +498,12 @@
     coeff = pl.pallas_call(
         functools.partial(coeff_body, arity),
         out_shape=[struct(rank, half)] * 2
+        + [struct(points, 3 * rank, dtype=BF16)]
         + [struct(points, depth, dtype=BF16)] * 2
         + [struct(depth, half, dtype=BF16)] * 4
         + [struct(rank, joined_width), struct(packed_rows, joined_width), struct(rank, joined_width)],
         in_specs=[pl.BlockSpec(memory_space=pltpu.SMEM)] + [pl.BlockSpec(memory_space=pl.ANY)] * len(large),
-        out_specs=[vmem] * 11,
+        out_specs=[vmem] * 12,
         scratch_shapes=[
             pltpu.VMEM((points, rank), F32),
             pltpu.VMEM((points, depth), F32),
@@ -432,34 +517,32 @@
             flops=6 * rank * depth * (points + 2 * half), bytes_accessed=14 << 20, transcendentals=0
         ),
     )
-    coeff_send, coeff_own, *halves, joined_mine, packed, mixed_mine = coeff(
+    coeff_send, coeff_own, basis_parts, *halves, joined_mine, packed, mixed_mine = coeff(
         ids, *[pltpu.with_memory_space_constraint(array, pltpu.HBM) for array in large]
     )
     inverse_parts, rhs_other, rhs_own = halves[:2], halves[2:4], halves[4:]
     coeff_got = swap_core(coeff_send)
 
-    near = swap_each(joined_mine, (1, 2))
-    mixed = swap_each(mixed_mine, (3, arity))
-    rest = swap_each(packed, (2 * arity, 3 * arity))
-
-    near_other = swap_core(near)
-    mixed_other = swap_core(mixed)
-    rest_other = swap_core(rest)
+    one = swap_each(mixed_mine, (1, arity))
+    two = swap_each(joined_mine, (2, 3))
+    three = swap_each(packed, (2 * arity, 3 * arity))
+    one_other = swap_core(one)
+    two_other = swap_core(two)
+    three_other = swap_core(three)
     joined, reduced_one = call(
         functools.partial(first_body, arity),
-        [struct(arity, rank, joined_width), struct(rank, couple)],
+        [struct(arity, rank, joined_width), struct(rank, 3 * couple, dtype=BF16)],
         [ids],
-        [joined_mine, near, near_other, mixed, mixed_other],
+        [joined_mine, one, one_other, two, two_other],
         6 * couple * rank * couple,
     )
-
     column_rows = arity * share + root_rows * (arity * wide // couple)
     column_half = -(-column_rows // 16) * 8
     column, column_part = call(
         functools.partial(column_body, arity, share, root_rows, wide),
         [struct(2 * column_half, joined_width), struct(column_half, joined_width)],
         [ids],
-        [packed, mixed, mixed_other, rest, rest_other],
+        [packed, one, one_other, three, three_other],
         0,
     )
     column_near = swap_each(column, (1, 2))
@@ -471,7 +554,7 @@
     pieces = [pieces[0]] + [swap(pieces[bits], bits) for bits in range(1, arity)]
     node_coeff, stack_one = call(
         functools.partial(node_up_body, arity),
-        [struct(rank, width), struct(couple, width)],
+        [struct(rank, width), struct(3 * couple, width, dtype=BF16)],
         [ids, leaf_slot],
         [reduced_one, *pieces],
         6 * rank * couple * width,
@@ -486,14 +569,14 @@
     )
 
     if tops == 1:
-        outs = [struct(rank, couple)]
+        outs = [struct(couple, 3 * couple, dtype=BF16)]
     else:
         outs = [struct(rank, joined_width), struct(rank, couple), struct(rank, wide)]
     second = call(
         functools.partial(second_body, arity, share, root_rows, wide),
         outs,
         [ids, node_slot],
-        [column, column_near, column_near_other, column_far, column_far_other],
+        [column, column_near, column_near_other, column_far, column_far_other, basis_rows],
         6 * couple * rank * couple,
         scratch=[pltpu.VMEM((couple, joined_width), F32), pltpu.VMEM((rank, wide), F32)],
     )
@@ -502,9 +585,9 @@
             functools.partial(down_body, arity),
             [struct(rank, width)] * arity,
             [ids, node_slot],
-            [second[0], node_solve, basis_rows, *uppers],
-            12 * rank * couple * width,
-            scratch=[pltpu.VMEM((couple, width), F32)],
+            [*second, node_solve, *uppers],
+            6 * couple * couple * width,
+            scratch=[pltpu.VMEM((3 * couple, width), BF16)],
         )
     else:
         mul = functools.partial(jnp.dot, precision=lax.Precision.HIGHEST)
@@ -533,25 +616,8 @@
 
     solve_got = swap_core(leaf_product(inverse_parts, rhs_other))
     base = leaf_product(inverse_parts, rhs_own, [solve_got])
-    return pl.pallas_call(
-        functools.partial(final_body, arity),
-        out_shape=struct(points, half),
-        grid_spec=pltpu.PrefetchScalarGridSpec(
-            num_scalar_prefetch=1,
-            grid=(arity,),
-            in_specs=[vmem] * (2 + arity),
-            out_specs=pl.BlockSpec((points, width), lambda i, ids: (0, (ids[0] % arity) ^ i)),
-            scratch_shapes=[
-                pltpu.VMEM((points, 2 * rank), BF16),
-                pltpu.VMEM((arity, 2 * rank, width), BF16),
-                pltpu.VMEM((arity, rank, width), BF16),
-            ],
-        ),
-        compiler_params=pltpu.CompilerParams(vmem_limit_bytes=16 << 20),
-        cost_estimate=pl.CostEstimate(
-            flops=6 * points * rank * half, bytes_accessed=8 * points * half, transcendentals=0
-        ),
-    )(ids, base, leaf_basis, *back)
+    so_far = final(ids, base, basis_parts, 0, back[:1])
+    return final(ids, base, basis_parts, 1, back[1:], so_far)
 
 
 def solution(mesh):

time: 81.2 us -> 77.9 us (0.959)
  waiting for transfers between devices: 31 us -> 28.1 us
    ppermute x4, waiting for transfers between devices: 13.1 us -> 11.2 us  [swap_each(): return lax.ppermute(block, ('leaf', 'rhs'), route)]
    ppermute x10, waiting for transfers between devices: 16.6 us -> 15.6 us  [swap(): lax.ppermute(block, 'leaf', [(low, low ^ bits) for low in range(count)])]
    ppermute x4, starting transfers between devices: 9.64 us -> 8.75 us  [swap_each(): return lax.ppermute(block, ('leaf', 'rhs'), route)]
    pallas_call x1 -> x2, Pallas kernels: 3.98 us -> 4.43 us  [final(): pl.pallas_call(functools.partial(final_body, first, half // width), out_s...]
  transfers between devices with their start and end apart: 21 -> 21, of which waited for: 9 -> 11; matrix products, arithmetic and copies ran while one was open for 0% -> 0% of each run, Pallas kernels for 13% -> 17%
where the time goes in v1:
time: 77.9 us; the launch traced here: 77.8 us
  waiting for transfers between devices  28.1 us (36%)
  starting transfers between devices  24.8 us (32%)
  Pallas kernels  24.6 us (32%)
    ppermute x10, waiting for transfers between devices, swap(): lax.ppermute(block, 'leaf', [(low, low ^ bits) for low in range(count)])  15.6 us
    pallas_call x9, Pallas kernels, call(): pl.pallas_call(body, out_shape=out_shapes, in_specs=[pl.BlockSpec(memory_...  15 us
    ppermute x10, starting transfers between devices, swap(): lax.ppermute(block, 'leaf', [(low, low ^ bits) for low in range(count)])  13.6 us
    ppermute x4, waiting for transfers between devices, swap_each(): return lax.ppermute(block, ('leaf', 'rhs'), route)  11.2 us
    ppermute x4, starting transfers between devices, swap_each(): return lax.ppermute(block, ('leaf', 'rhs'), route)  8.75 us
    pallas_call x1, Pallas kernels, per_device(): coeff(ids, *[pltpu.with_memory_space_constraint(array, pltpu.HBM) for arr...  5.22 us
    pallas_call x2, Pallas kernels, final(): pl.pallas_call(functools.partial(final_body, first, half // width), out_s...  4.43 us
    ppermute x7, starting transfers between devices, swap_core(): return lax.ppermute(block, 'rhs', [(0, 1), (1, 0)])  2.46 us
  transfers between devices with their start and end apart: 21, of which 11 were waited for; matrix products, arithmetic and copies ran while one was open for 0% of the time, Pallas kernels for 17%

profile of v1, /device:TPU:0, one launch (start us, length us, event | category | flops | bytes accessed | tf_op | source)
XLA Modules:
  0.0 77.8 jit_solution(5039876729171423993)
XLA Ops:
  0.0 0.1 pad_add_fusion.ids
  0.1 5.2 %shard_map.100 = (f32[128,1024]{1,0:T(8,128)S(1)}, f32[128,1024]{1,0:T(8,128)S(1)}, bf16[1024,384]{1,0:T(8,128)(2,1)S(1)}, bf16[1024,512]{1,0:T(8,128)(2,1)S(1)}...) custom-call(s32[2]{0:T(128)S(1)} %pad_add_fusion.ids, ...), custom_call_target="tpu_custom_call" | custom-call | flops 1207959552 | bytes 14680064 | tf_op jit(solution)/shard_map/pallas_call | solution.py:520
  5.3 0.0 copy-start.1
  5.3 3.9 %shard_map.101 = f32[1024,1024]{1,0:T(8,128)S(1)} custom-call(bf16[1024,512]{1,0:T(8,128)(2,1)S(1)} %get-tuple-element.33.inverse_high, bf16[1024,512]{1,0:T(8,128)(2,1)S(1)} %get-tuple-element.34.inverse_low, bf16[512,1024]{1,0:T(8,128)(2,1)S(1)} %get-tuple-element.37.rhs_high, bf16[512,1024]{1,0:T(8,128)(2,1)S(1)} %get-tuple-element.38.rhs_low), custom_call_target="tpu_custom_call" | custom-call | flops 3221225472 | bytes 8388608 | tf_op jit(solution)/shard_map/pallas_call | solution.py:37
  9.2 0.0 copy-start
  9.2 0.6 collective-permute-start
  9.8 2.6 %collective-permute-start.1 = (f32[128,640]{1,0:T(8,128)S(1)}, f32[128,640]{1,0:T(8,128)S(1)}, u32[]{:S(2)}, u32[]{:S(2)}) collective-permute-start(f32[128,640]{1,0:T(8,128)S(1)} %get-tuple-element.41), channel_id=1, source_target_pairs={{0,2},{1,9},{2,0},{3,11},{4,6},{5,13},{6,4},{7,15},{8,10},{9,1},{1... | collective-permute-start | bytes 983048 | tf_op jit(solution)/shard_map/ppermute | solution.py:464
  12.4 5.1 %collective-permute-done.1.one = f32[128,640]{1,0:T(8,128)S(1)} collective-permute-done((f32[128,640]{1,0:T(8,128)S(1)}, f32[128,640]{1,0:T(8,128)S(1)}, u32[]{:S(2)}, u32[]{:S(2)}) %collective-permute-start.1) | collective-permute-done | bytes 327712 | tf_op jit(solution)/shard_map/ppermute | solution.py:464
  17.4 0.0 collective-permute-start.2
  17.4 3.1 %collective-permute-start.3 = (f32[40,640]{1,0:T(8,128)S(1)}, f32[40,640]{1,0:T(8,128)S(1)}, u32[]{:S(2)}, u32[]{:S(2)}) collective-permute-start(f32[40,640]{1,0:T(8,128)S(1)} %get-tuple-element.40.packed), channel_id=1, source_target_pairs={{0,16},{1,25},{2,18},{3,27},{4,20},{5,29},{6,22},{7,31},{8,24},{9,... | collective-permute-start | bytes 307208 | tf_op jit(solution)/shard_map/ppermute | solution.py:464
  20.5 1.5 %collective-permute-start.9 = (f32[128,640]{1,0:T(8,128)S(1)}, f32[128,640]{1,0:T(8,128)S(1)}, u32[]{:S(2)}, u32[]{:S(2)}) collective-permute-start(f32[128,640]{1,0:T(8,128)S(1)} %get-tuple-element.44.mine), channel_id=1, source_target_pairs={{0,4},{1,7},{2,6},{3,5},{4,0},{5,3},{6,2},{7,1},{8,12},{9,15},{10,... | collective-permute-start | bytes 983048 | tf_op jit(solution)/shard_map/ppermute | solution.py:464
  22.1 1.9 %collective-permute-start.11 = (f32[128,1024]{1,0:T(8,128)S(1)}, f32[128,1024]{1,0:T(8,128)S(1)}, u32[]{:S(2)}, u32[]{:S(2)}) collective-permute-start(f32[128,1024]{1,0:T(8,128)S(1)} %get-tuple-element.48), channel_id=1, source_target_pairs={{0,1},{1,0},{2,3},{3,2},{4,5},{5,4},{6,7},{7,6},{8,9},{9,8},{10,11... | collective-permute-start | bytes 1572872 | tf_op jit(solution)/shard_map/ppermute | solution.py:453
  23.9 2.5 %collective-permute-done.3.three = f32[40,640]{1,0:T(8,128)S(1)} collective-permute-done((f32[40,640]{1,0:T(8,128)S(1)}, f32[40,640]{1,0:T(8,128)S(1)}, u32[]{:S(2)}, u32[]{:S(2)}) %collective-permute-start.3) | collective-permute-done | bytes 102432 | tf_op jit(solution)/shard_map/ppermute | solution.py:464
  26.4 0.0 collective-permute-start.4
  26.4 1.3 %collective-permute-done.4.three_other = f32[40,640]{1,0:T(8,128)S(1)} collective-permute-done((f32[40,640]{1,0:T(8,128)S(1)}, f32[40,640]{1,0:T(8,128)S(1)}, u32[]{:S(2)}, u32[]{:S(2)}) %collective-permute-start.4) | collective-permute-done | bytes 102432 | tf_op jit(solution)/shard_map/ppermute | solution.py:453
  27.8 0.0 collective-permute-done.2.one_other
  27.8 0.6 shard_map.103
  28.4 1.6 %collective-permute-start.5 = (f32[144,640]{1,0:T(8,128)S(1)}, f32[144,640]{1,0:T(8,128)S(1)}, u32[]{:S(2)}, u32[]{:S(2)}) collective-permute-start(f32[144,640]{1,0:T(8,128)S(1)} %get-tuple-element.42.mine), channel_id=1, source_target_pairs={{0,2},{1,5},{2,0},{3,7},{4,6},{5,1},{6,4},{7,3},{8,10},{9,13},{10,... | collective-permute-start | bytes 1105928 | tf_op jit(solution)/shard_map/ppermute | solution.py:464
  29.9 1.2 %collective-permute-done.9.two = f32[128,640]{1,0:T(8,128)S(1)} collective-permute-done((f32[128,640]{1,0:T(8,128)S(1)}, f32[128,640]{1,0:T(8,128)S(1)}, u32[]{:S(2)}, u32[]{:S(2)}) %collective-permute-start.9) | collective-permute-done | bytes 327712 | tf_op jit(solution)/shard_map/ppermute | solution.py:464
  31.1 0.0 collective-permute-start.10
  31.1 2.4 %collective-permute-start.7 = (f32[72,640]{1,0:T(8,128)S(1)}, f32[72,640]{1,0:T(8,128)S(1)}, u32[]{:S(2)}, u32[]{:S(2)}) collective-permute-start(f32[72,640]{1,0:T(8,128)S(1)} %get-tuple-element.43), channel_id=1, source_target_pairs={{0,6},{2,4},{4,2},{6,0},{8,14},{10,12},{12,10},{14,8},{16,22},{18,... | collective-permute-start | bytes 552968 | tf_op jit(solution)/shard_map/ppermute | solution.py:449
  33.6 0.0 collective-permute-done.11.got
  33.6 0.1 shard_map.105
  33.6 0.6 collective-permute-start.12
  34.2 2.5 %collective-permute-done.5.near = f32[144,640]{1,0:T(8,128)S(1)} collective-permute-done((f32[144,640]{1,0:T(8,128)S(1)}, f32[144,640]{1,0:T(8,128)S(1)}, u32[]{:S(2)}, u32[]{:S(2)}) %collective-permute-start.5) | collective-permute-done | bytes 368672 | tf_op jit(solution)/shard_map/ppermute | solution.py:464
  36.7 0.0 collective-permute-start.6
  36.7 5.5 %collective-permute-done.7.far = f32[72,640]{1,0:T(8,128)S(1)} collective-permute-done((f32[72,640]{1,0:T(8,128)S(1)}, f32[72,640]{1,0:T(8,128)S(1)}, u32[]{:S(2)}, u32[]{:S(2)}) %collective-permute-start.7) | collective-permute-done | bytes 184352 | tf_op jit(solution)/shard_map/ppermute | solution.py:449
  42.3 0.0 collective-permute-start.8
  42.3 0.0 collective-permute-done.10.two_other
  42.3 0.0 collective-permute-start.13
  42.3 0.4 collective-permute-done.12.refs_1_
  42.7 2.5 %collective-permute-start.14 = (f32[128,256]{1,0:T(8,128)S(1)}, f32[128,256]{1,0:T(8,128)S(1)}, u32[]{:S(2)}, u32[]{:S(2)}) collective-permute-start(f32[128,256]{1,0:T(8,128)S(1)} %get-tuple-element.52), channel_id=1, source_target_pairs={{0,6},{2,4},{4,2},{6,0},{8,14},{10,12},{12,10},{14,8},{16,22},{18,... | collective-permute-start | bytes 393224 | tf_op jit(solution)/shard_map/ppermute | solution.py:449
  45.2 1.1 %shard_map.104 = (f32[4,128,640]{2,1,0:T(8,128)S(1)}, bf16[128,1536]{1,0:T(8,128)(2,1)S(1)}) custom-call(s32[2]{0:T(128)S(1)} %pad_add_fusion.ids, f32[128,640]{1,0:T(8,128)S(1)} %get-tuple-element.44.mine, f32[128,640]{1,0:T(8,128)S(1)} %collective-permute-done.1.one, f32[128,640]{1,0:T(8,128)S(1)} %collective-permute-done.2.one_other, ...), custom_call_target="tpu_custom_call" | custom-call | flops 201326592 | bytes 3342336 | tf_op jit(solution)/shard_map/pallas_call | solution.py:37
  46.3 4.7 %collective-permute-done.13.refs_2_ = f32[128,256]{1,0:T(8,128)S(1)} collective-permute-done((f32[128,256]{1,0:T(8,128)S(1)}, f32[128,256]{1,0:T(8,128)S(1)}, u32[]{:S(2)}, u32[]{:S(2)}) %collective-permute-start.13) | collective-permute-done | bytes 131104 | tf_op jit(solution)/shard_map/ppermute | solution.py:449
  51.0 0.0 collective-permute-done.14.refs_3_
  51.0 0.0 copy-done.1
  51.0 0.9 %shard_map.106 = (f32[128,256]{1,0:T(8,128)S(1)}, bf16[1536,256]{1,0:T(8,128)(2,1)S(1)}) custom-call(s32[2]{0:T(128)S(1)} %pad_add_fusion.ids, s32[16]{0:T(128)S(1)} %copy-done.1, bf16[128,1536]{1,0:T(8,128)(2,1)S(1)} %get-tuple-element.46.reduced, f32[128,256]{1,0:T(8,128)S(1)} %get-tuple-element.49.refs_0_, ...), custom_call_target="tpu_custom_call" | custom-call | flops 100663296 | bytes 1835008 | tf_op jit(solution)/shard_map/pallas_call | solution.py:37
  51.9 2.8 %collective-permute-start.17 = (f32[128,256]{1,0:T(8,128)S(1)}, f32[128,256]{1,0:T(8,128)S(1)}, u32[]{:S(2)}, u32[]{:S(2)}) collective-permute-start(f32[128,256]{1,0:T(8,128)S(1)} %get-tuple-element.56.refs_0_), channel_id=1, source_target_pairs={{0,24},{2,26},{4,28},{6,30},{8,16},{10,18},{12,20},{14,22},{16,8},... | collective-permute-start | bytes 393224 | tf_op jit(solution)/shard_map/ppermute | solution.py:449
  54.7 0.0 collective-permute-start.16
  54.7 0.0 collective-permute-done.8.far_other
  54.7 1.6 %collective-permute-start.15 = (f32[128,256]{1,0:T(8,128)S(1)}, f32[128,256]{1,0:T(8,128)S(1)}, u32[]{:S(2)}, u32[]{:S(2)}) collective-permute-start(f32[128,256]{1,0:T(8,128)S(1)} %get-tuple-element.56.refs_0_), channel_id=1, source_target_pairs={{0,8},{2,10},{4,12},{6,14},{8,0},{10,2},{12,4},{14,6},{16,24},{18,... | collective-permute-start | bytes 393224 | tf_op jit(solution)/shard_map/ppermute | solution.py:449
  56.4 1.1 %shard_map.107 = (f32[512,256]{1,0:T(8,128)S(1)}, f32[512,128]{1,0:T(8,128)S(1)}) custom-call(s32[2]{0:T(128)S(1)} %pad_add_fusion.ids, s32[16]{0:T(128)S(1)} %copy-done.1, f32[4,128,640]{2,1,0:T(8,128)S(1)} %get-tuple-element.45.joined, bf16[1536,256]{1,0:T(8,128)(2,1)S(1)} %get-tuple-element.53.stack), custom_call_target="tpu_custom_call" | custom-call | flops 402653184 | bytes 2883584 | tf_op jit(solution)/shard_map/pallas_call | solution.py:37
  57.5 0.0 collective-permute-done.6.near_other
  57.5 0.0 copy-done
  57.5 2.1 %shard_map.108.down_map = bf16[512,1536]{1,0:T(8,128)(2,1)S(1)} custom-call(s32[2]{0:T(128)S(1)} %pad_add_fusion.ids, s32[4]{0:T(128)S(1)} %copy-done, f32[144,640]{1,0:T(8,128)S(1)} %get-tuple-element.42.mine, f32[144,640]{1,0:T(8,128)S(1)} %collective-permute-done.5.near, f32[144,640]{1,0:T(8,128)S(1)} %collective-permute-done.6.near_other, ...), custom_call_target="tpu_custom_call" | custom-call | flops 201326592 | bytes 3309568 | tf_op jit(solution)/shard_map/pallas_call | solution.py:37
  59.7 0.6 collective-permute-done.17.refs_3_
  60.3 4.2 %collective-permute-done.16.refs_2_ = f32[128,256]{1,0:T(8,128)S(1)} collective-permute-done((f32[128,256]{1,0:T(8,128)S(1)}, f32[128,256]{1,0:T(8,128)S(1)}, u32[]{:S(2)}, u32[]{:S(2)}) %collective-permute-start.16) | collective-permute-done | bytes 131104 | tf_op jit(solution)/shard_map/ppermute | solution.py:449
  64.5 0.0 collective-permute-done.15.refs_1_
  64.5 1.2 %shard_map.109 = (f32[128,256]{1,0:T(8,128)S(1)}, f32[128,256]{1,0:T(8,128)S(1)}, f32[128,256]{1,0:T(8,128)S(1)}, f32[128,256]{1,0:T(8,128)S(1)}) custom-call(s32[2]{0:T(128)S(1)} %pad_add_fusion.ids, s32[4]{0:T(128)S(1)} %copy-done, bf16[512,1536]{1,0:T(8,128)(2,1)S(1)} %shard_map.108.down_map, f32[512,256]{1,0:T(8,128)S(1)} %get-tuple-element.55.solve, ...), custom_call_target="tpu_custom_call" | custom-call | flops 402653184 | bytes 3145728 | tf_op jit(solution)/shard_map/pallas_call | solution.py:37
  65.7 1.6 %collective-permute-start.18 = (f32[128,256]{1,0:T(8,128)S(1)}, f32[128,256]{1,0:T(8,128)S(1)}, u32[]{:S(2)}, u32[]{:S(2)}) collective-permute-start(f32[128,256]{1,0:T(8,128)S(1)} %get-tuple-element.57), channel_id=1, source_target_pairs={{0,2},{2,0},{4,6},{6,4},{8,10},{10,8},{12,14},{14,12},{16,18},{18,... | collective-permute-start | bytes 393224 | tf_op jit(solution)/shard_map/ppermute | solution.py:449
  67.3 0.5 collective-permute-start.19
  67.8 1.4 %collective-permute-start.20 = (f32[128,256]{1,0:T(8,128)S(1)}, f32[128,256]{1,0:T(8,128)S(1)}, u32[]{:S(2)}, u32[]{:S(2)}) collective-permute-start(f32[128,256]{1,0:T(8,128)S(1)} %get-tuple-element.59), channel_id=1, source_target_pairs={{0,6},{2,4},{4,2},{6,0},{8,14},{10,12},{12,10},{14,8},{16,22},{18,... | collective-permute-start | bytes 393224 | tf_op jit(solution)/shard_map/ppermute | solution.py:449
  69.2 0.0 collective-permute-done.rest_0_
  69.2 3.9 %shard_map.102.base = f32[1024,1024]{1,0:T(8,128)S(1)} custom-call(bf16[1024,512]{1,0:T(8,128)(2,1)S(1)} %get-tuple-element.33.inverse_high, bf16[1024,512]{1,0:T(8,128)(2,1)S(1)} %get-tuple-element.34.inverse_low, bf16[512,1024]{1,0:T(8,128)(2,1)S(1)} %get-tuple-element.35.rhs_high, bf16[512,1024]{1,0:T(8,128)(2,1)S(1)} %get-tuple-element.36.rhs_low, ...), custom_call_target="tpu_custom_call" | custom-call | flops 3221225472 | bytes 12582912 | tf_op jit(solution)/shard_map/pallas_call | solution.py:37
  73.2 1.8 %shard_map.110.refs_3_ = f32[1024,1024]{1,0:T(8,128)} custom-call(s32[2]{0:T(128)S(1)} %pad_add_fusion.ids, f32[1024,1024]{1,0:T(8,128)S(1)} %shard_map.102.base, bf16[1024,384]{1,0:T(8,128)(2,1)S(1)} %get-tuple-element.39.left, f32[128,256]{1,0:T(8,128)S(1)} %get-tuple-element.60.refs_0_), custom_call_target="tpu_custom_call" | custom-call | flops 201326592 | bytes 2097152 | tf_op jit(solution)/shard_map/pallas_call | solution.py:427
  75.0 0.0 collective-permute-done.18.refs_0_
  75.0 0.2 collective-permute-done.19.refs_1_
  75.2 0.0 collective-permute-done.20.refs_2_
  75.2 2.6 %shard_map.111 = f32[1024,1024]{1,0:T(8,128)} custom-call(s32[2]{0:T(128)S(1)} %pad_add_fusion.ids, f32[1024,1024]{1,0:T(8,128)S(1)} %shard_map.102.base, bf16[1024,384]{1,0:T(8,128)(2,1)S(1)} %get-tuple-element.39.left, f32[128,256]{1,0:T(8,128)S(1)} %collective-permute-done.18.refs_0_, ...), custom_call_target="tpu_custom_call", output_to_operand_aliasing={{}: (6, {})} | custom-call | flops 603979776 | bytes 6291456 | tf_op jit(solution)/shard_map/pallas_call | solution.py:427
Async XLA Ops:
  5.3 45.7 %copy-start.1 = (s32[16]{0:T(128)S(1)}, s32[16]{0:T(128)}, u32[]{:S(2)}) copy-start(s32[16]{0:T(128)} %slots.3) | copy-start | bytes 196
  9.2 48.3 %copy-start = (s32[4]{0:T(128)S(1)}, s32[4]{0:T(128)}, u32[]{:S(2)}) copy-start(s32[4]{0:T(128)} %node_slots.3) | copy-start | bytes 52
  9.2 60.0 %collective-permute-start = (f32[1024,1024]{1,0:T(8,128)S(1)}, f32[1024,1024]{1,0:T(8,128)S(1)}, u32[]{:S(2)}, u32[]{:S(2)}) collective-permute-start(f32[1024,1024]{1,0:T(8,128)S(1)} %shard_map.101), channel_id=1, source_target_pairs={{0,1},{1,0},{2,3},{3,2},{4,5},{5,4},{6,7},{7,6},{8,9},{9,8},{10,11... | collective-permute-start | bytes 12582920 | tf_op jit(solution)/shard_map/ppermute | solution.py:453
  9.8 7.6 %collective-permute-start.1 = (f32[128,640]{1,0:T(8,128)S(1)}, f32[128,640]{1,0:T(8,128)S(1)}, u32[]{:S(2)}, u32[]{:S(2)}) collective-permute-start(f32[128,640]{1,0:T(8,128)S(1)} %get-tuple-element.41), channel_id=1, source_target_pairs={{0,2},{1,9},{2,0},{3,11},{4,6},{5,13},{6,4},{7,15},{8,10},{9,1},{1... | collective-permute-start | bytes 983048 | tf_op jit(solution)/shard_map/ppermute | solution.py:464
  17.4 10.3 %collective-permute-start.2 = (f32[128,640]{1,0:T(8,128)S(1)}, f32[128,640]{1,0:T(8,128)S(1)}, u32[]{:S(2)}, u32[]{:S(2)}) collective-permute-start(f32[128,640]{1,0:T(8,128)S(1)} %collective-permute-done.1.one), channel_id=1, source_target_pairs={{0,1},{1,0},{2,3},{3,2},{4,5},{5,4},{6,7},{7,6},{8,9},{9,8},{10,11... | collective-permute-start | bytes 983048 | tf_op jit(solution)/shard_map/ppermute | solution.py:453
  17.4 9.0 %collective-permute-start.3 = (f32[40,640]{1,0:T(8,128)S(1)}, f32[40,640]{1,0:T(8,128)S(1)}, u32[]{:S(2)}, u32[]{:S(2)}) collective-permute-start(f32[40,640]{1,0:T(8,128)S(1)} %get-tuple-element.40.packed), channel_id=1, source_target_pairs={{0,16},{1,25},{2,18},{3,27},{4,20},{5,29},{6,22},{7,31},{8,24},{9,... | collective-permute-start | bytes 307208 | tf_op jit(solution)/shard_map/ppermute | solution.py:464
  20.5 10.6 %collective-permute-start.9 = (f32[128,640]{1,0:T(8,128)S(1)}, f32[128,640]{1,0:T(8,128)S(1)}, u32[]{:S(2)}, u32[]{:S(2)}) collective-permute-start(f32[128,640]{1,0:T(8,128)S(1)} %get-tuple-element.44.mine), channel_id=1, source_target_pairs={{0,4},{1,7},{2,6},{3,5},{4,0},{5,3},{6,2},{7,1},{8,12},{9,15},{10,... | collective-permute-start | bytes 983048 | tf_op jit(solution)/shard_map/ppermute | solution.py:464
  22.1 11.5 %collective-permute-start.11 = (f32[128,1024]{1,0:T(8,128)S(1)}, f32[128,1024]{1,0:T(8,128)S(1)}, u32[]{:S(2)}, u32[]{:S(2)}) collective-permute-start(f32[128,1024]{1,0:T(8,128)S(1)} %get-tuple-element.48), channel_id=1, source_target_pairs={{0,1},{1,0},{2,3},{3,2},{4,5},{5,4},{6,7},{7,6},{8,9},{9,8},{10,11... | collective-permute-start | bytes 1572872 | tf_op jit(solution)/shard_map/ppermute | solution.py:453
  26.4 1.3 %collective-permute-start.4 = (f32[40,640]{1,0:T(8,128)S(1)}, f32[40,640]{1,0:T(8,128)S(1)}, u32[]{:S(2)}, u32[]{:S(2)}) collective-permute-start(f32[40,640]{1,0:T(8,128)S(1)} %collective-permute-done.3.three), channel_id=1, source_target_pairs={{0,1},{1,0},{2,3},{3,2},{4,5},{5,4},{6,7},{7,6},{8,9},{9,8},{10,11... | collective-permute-start | bytes 307208 | tf_op jit(solution)/shard_map/ppermute | solution.py:453
  28.4 8.4 %collective-permute-start.5 = (f32[144,640]{1,0:T(8,128)S(1)}, f32[144,640]{1,0:T(8,128)S(1)}, u32[]{:S(2)}, u32[]{:S(2)}) collective-permute-start(f32[144,640]{1,0:T(8,128)S(1)} %get-tuple-element.42.mine), channel_id=1, source_target_pairs={{0,2},{1,5},{2,0},{3,7},{4,6},{5,1},{6,4},{7,3},{8,10},{9,13},{10,... | collective-permute-start | bytes 1105928 | tf_op jit(solution)/shard_map/ppermute | solution.py:464
  31.1 11.2 %collective-permute-start.10 = (f32[128,640]{1,0:T(8,128)S(1)}, f32[128,640]{1,0:T(8,128)S(1)}, u32[]{:S(2)}, u32[]{:S(2)}) collective-permute-start(f32[128,640]{1,0:T(8,128)S(1)} %collective-permute-done.9.two), channel_id=1, source_target_pairs={{0,1},{1,0},{2,3},{3,2},{4,5},{5,4},{6,7},{7,6},{8,9},{9,8},{10,11... | collective-permute-start | bytes 983048 | tf_op jit(solution)/shard_map/ppermute | solution.py:453
  31.1 11.1 %collective-permute-start.7 = (f32[72,640]{1,0:T(8,128)S(1)}, f32[72,640]{1,0:T(8,128)S(1)}, u32[]{:S(2)}, u32[]{:S(2)}) collective-permute-start(f32[72,640]{1,0:T(8,128)S(1)} %get-tuple-element.43), channel_id=1, source_target_pairs={{0,6},{2,4},{4,2},{6,0},{8,14},{10,12},{12,10},{14,8},{16,22},{18,... | collective-permute-start | bytes 552968 | tf_op jit(solution)/shard_map/ppermute | solution.py:449
  33.6 9.1 %collective-permute-start.12 = (f32[128,256]{1,0:T(8,128)S(1)}, f32[128,256]{1,0:T(8,128)S(1)}, u32[]{:S(2)}, u32[]{:S(2)}) collective-permute-start(f32[128,256]{1,0:T(8,128)S(1)} %get-tuple-element.50), channel_id=1, source_target_pairs={{0,2},{2,0},{4,6},{6,4},{8,10},{10,8},{12,14},{14,12},{16,18},{18,... | collective-permute-start | bytes 393224 | tf_op jit(solution)/shard_map/ppermute | solution.py:449
  36.7 20.8 %collective-permute-start.6 = (f32[144,640]{1,0:T(8,128)S(1)}, f32[144,640]{1,0:T(8,128)S(1)}, u32[]{:S(2)}, u32[]{:S(2)}) collective-permute-start(f32[144,640]{1,0:T(8,128)S(1)} %collective-permute-done.5.near), channel_id=1, source_target_pairs={{0,1},{1,0},{2,3},{3,2},{4,5},{5,4},{6,7},{7,6},{8,9},{9,8},{10,11... | collective-permute-start | bytes 1105928 | tf_op jit(solution)/shard_map/ppermute | solution.py:453
  42.3 12.5 %collective-permute-start.8 = (f32[72,640]{1,0:T(8,128)S(1)}, f32[72,640]{1,0:T(8,128)S(1)}, u32[]{:S(2)}, u32[]{:S(2)}) collective-permute-start(f32[72,640]{1,0:T(8,128)S(1)} %collective-permute-done.7.far), channel_id=1, source_target_pairs={{0,1},{1,0},{2,3},{3,2},{4,5},{5,4},{6,7},{7,6},{8,9},{9,8},{10,11... | collective-permute-start | bytes 552968 | tf_op jit(solution)/shard_map/ppermute | solution.py:453
  42.3 8.7 %collective-permute-start.13 = (f32[128,256]{1,0:T(8,128)S(1)}, f32[128,256]{1,0:T(8,128)S(1)}, u32[]{:S(2)}, u32[]{:S(2)}) collective-permute-start(f32[128,256]{1,0:T(8,128)S(1)} %get-tuple-element.51), channel_id=1, source_target_pairs={{0,4},{2,6},{4,0},{6,2},{8,12},{10,14},{12,8},{14,10},{16,20},{18,... | collective-permute-start | bytes 393224 | tf_op jit(solution)/shard_map/ppermute | solution.py:449
  42.7 8.3 %collective-permute-start.14 = (f32[128,256]{1,0:T(8,128)S(1)}, f32[128,256]{1,0:T(8,128)S(1)}, u32[]{:S(2)}, u32[]{:S(2)}) collective-permute-start(f32[128,256]{1,0:T(8,128)S(1)} %get-tuple-element.52), channel_id=1, source_target_pairs={{0,6},{2,4},{4,2},{6,0},{8,14},{10,12},{12,10},{14,8},{16,22},{18,... | collective-permute-start | bytes 393224 | tf_op jit(solution)/shard_map/ppermute | solution.py:449
  51.9 8.3 %collective-permute-start.17 = (f32[128,256]{1,0:T(8,128)S(1)}, f32[128,256]{1,0:T(8,128)S(1)}, u32[]{:S(2)}, u32[]{:S(2)}) collective-permute-start(f32[128,256]{1,0:T(8,128)S(1)} %get-tuple-element.56.refs_0_), channel_id=1, source_target_pairs={{0,24},{2,26},{4,28},{6,30},{8,16},{10,18},{12,20},{14,22},{16,8},... | collective-permute-start | bytes 393224 | tf_op jit(solution)/shard_map/ppermute | solution.py:449
  54.7 9.7 %collective-permute-start.16 = (f32[128,256]{1,0:T(8,128)S(1)}, f32[128,256]{1,0:T(8,128)S(1)}, u32[]{:S(2)}, u32[]{:S(2)}) collective-permute-start(f32[128,256]{1,0:T(8,128)S(1)} %get-tuple-element.56.refs_0_), channel_id=1, source_target_pairs={{0,16},{2,18},{4,20},{6,22},{8,24},{10,26},{12,28},{14,30},{16,0},... | collective-permute-start | bytes 393224 | tf_op jit(solution)/shard_map/ppermute | solution.py:449
  54.7 9.7 %collective-permute-start.15 = (f32[128,256]{1,0:T(8,128)S(1)}, f32[128,256]{1,0:T(8,128)S(1)}, u32[]{:S(2)}, u32[]{:S(2)}) collective-permute-start(f32[128,256]{1,0:T(8,128)S(1)} %get-tuple-element.56.refs_0_), channel_id=1, source_target_pairs={{0,8},{2,10},{4,12},{6,14},{8,0},{10,2},{12,4},{14,6},{16,24},{18,... | collective-permute-start | bytes 393224 | tf_op jit(solution)/shard_map/ppermute | solution.py:449
  65.7 9.3 %collective-permute-start.18 = (f32[128,256]{1,0:T(8,128)S(1)}, f32[128,256]{1,0:T(8,128)S(1)}, u32[]{:S(2)}, u32[]{:S(2)}) collective-permute-start(f32[128,256]{1,0:T(8,128)S(1)} %get-tuple-element.57), channel_id=1, source_target_pairs={{0,2},{2,0},{4,6},{6,4},{8,10},{10,8},{12,14},{14,12},{16,18},{18,... | collective-permute-start | bytes 393224 | tf_op jit(solution)/shard_map/ppermute | solution.py:449
  67.3 7.9 %collective-permute-start.19 = (f32[128,256]{1,0:T(8,128)S(1)}, f32[128,256]{1,0:T(8,128)S(1)}, u32[]{:S(2)}, u32[]{:S(2)}) collective-permute-start(f32[128,256]{1,0:T(8,128)S(1)} %get-tuple-element.58), channel_id=1, source_target_pairs={{0,4},{2,6},{4,0},{6,2},{8,12},{10,14},{12,8},{14,10},{16,20},{18,... | collective-permute-start | bytes 393224 | tf_op jit(solution)/shard_map/ppermute | solution.py:449
  67.8 7.4 %collective-permute-start.20 = (f32[128,256]{1,0:T(8,128)S(1)}, f32[128,256]{1,0:T(8,128)S(1)}, u32[]{:S(2)}, u32[]{:S(2)}) collective-permute-start(f32[128,256]{1,0:T(8,128)S(1)} %get-tuple-element.59), channel_id=1, source_target_pairs={{0,6},{2,4},{4,2},{6,0},{8,14},{10,12},{12,10},{14,8},{16,22},{18,... | collective-permute-start | bytes 393224 | tf_op jit(solution)/shard_map/ppermute | solution.py:449

commit v2 on v1

--- a/solution.py
+++ b/solution.py
@@ -49,56 +49,48 @@
     return jax.ShapeDtypeStruct(shape, dtype)
 
 
+def pack_body(ids, couple_one, basis_one, couple_two, basis_two, root, joined, packed, mixed, sems):
+    couple = couple_one.shape[1]
+    share = couple_two.shape[0]
+    root_rows, wide = root.shape
+    piece = min(wide, couple)
+    moves = [
+        (couple_one, joined.at[:, :couple]),
+        (basis_one, joined.at[:, couple:]),
+        (couple_two, packed.at[:share, :couple]),
+        (basis_two, packed.at[:share, couple:]),
+    ]
+    for part in range(wide // piece):
+        low = share + part * root_rows
+        moves.append(
+            (root.at[:, part * piece : (part + 1) * piece], packed.at[low : low + root_rows, :piece])
+        )
+    copies = [pltpu.make_async_copy(*move, sems.at[number]) for number, move in enumerate(moves)]
+    for copy in copies:
+        copy.start()
+    packed[share:, piece:] = jnp.zeros_like(packed[share:, piece:])
+    for copy in copies:
+        copy.wait()
+
+    @pl.when(ids[1] == 0)
+    def _():
+        mixed[...] = joined[...]
+
+    @pl.when(ids[1] != 0)
+    def _():
+        mixed[: packed.shape[0]] = packed[...]
+        mixed[packed.shape[0] :] = jnp.zeros_like(mixed[packed.shape[0] :])
+
+
 def coeff_body(
-    arity, ids, basis, inverse, rhs, couple_one, basis_one, couple_two, basis_two, root,
-    send, own, basis_parts, inverse_high, inverse_low, other_high, other_low, own_high, own_low, joined, packed, mixed,
-    basis_here, inverse_here, rhs_here, turned, projected, sems,
+    arity, ids, basis, inverse, rhs,
+    send, own, basis_parts, inverse_high, inverse_low, other_high, other_low, own_high, own_low,
+    turned, projected,
 ):
     member, core = ids[0] % arity, ids[1]
     rank, half = send.shape
     width = half // arity
-    couple = couple_one.shape[1]
-    share = couple_two.shape[0]
-    root_rows, wide = root.shape
-    piece = min(wide, couple)
     chunk = basis.shape[0] // arity
-    count = iter(range(sems.shape[0]))
-
-    def fetch(source, target):
-        copy = pltpu.make_async_copy(source, target, sems.at[next(count)])
-        copy.start()
-        return copy
-
-    basis_copy = fetch(basis, basis_here)
-    inverse_copies = [
-        fetch(inverse.at[step * chunk : (step + 1) * chunk], inverse_here.at[step * chunk : (step + 1) * chunk])
-        for step in range(arity)
-    ]
-    rhs_copies = []
-    for side in range(2):
-        for bits in range(arity):
-            column = (((1 - core) if side == 0 else core) * arity + (member ^ bits)) * width
-            at = (side * arity + bits) * width
-            rhs_copies.append(
-                fetch(rhs.at[:, pl.ds(pl.multiple_of(column, width), width)], rhs_here.at[:, at : at + width])
-            )
-            if side == 0 and bits == arity - 1:
-                matrix_copies = [
-                    fetch(couple_one, joined.at[:, :couple]),
-                    fetch(basis_one, joined.at[:, couple:]),
-                    fetch(couple_two, packed.at[:share, :couple]),
-                    fetch(basis_two, packed.at[:share, couple:]),
-                ]
-                for part in range(wide // piece):
-                    low = share + part * root_rows
-                    matrix_copies.append(
-                        fetch(
-                            root.at[:, part * piece : (part + 1) * piece],
-                            packed.at[low : low + root_rows, :piece],
-                        )
-                    )
-
-    packed[share:, piece:] = jnp.zeros_like(packed[share:, piece:])
 
     def parts(source, rows, columns, out_high, out_low, out_columns):
         for low_row in range(rows.start, rows.stop, 64):
@@ -107,11 +99,10 @@
             out_high[at, out_columns] = high
             out_low[at, out_columns] = low
 
-    basis_copy.wait()
     points = basis.shape[0]
     for low_row in range(0, points, rank):
         at = slice(low_row, low_row + rank)
-        value = basis_here[at]
+        value = basis[at]
         high, low = split(value)
         basis_parts[at, :rank] = high
         basis_parts[at, rank : 2 * rank] = low
@@ -120,10 +111,9 @@
         turned[:rank, at] = high
         turned[rank:, at] = low
     for step in range(arity):
-        inverse_copies[step].wait()
         everything = slice(0, inverse.shape[1])
         parts(
-            inverse_here, slice(step * chunk, (step + 1) * chunk), everything, inverse_high, inverse_low, everything
+            inverse, slice(step * chunk, (step + 1) * chunk), everything, inverse_high, inverse_low, everything
         )
     depth = inverse.shape[1]
     blocks = [
@@ -134,9 +124,9 @@
 
     def prepare(number):
         side, bits, _, out_high, out_low = blocks[number]
-        at = (side * arity + bits) * width
+        place = (((1 - core) if side == 0 else core) * arity + (member ^ bits)) * width
         columns = slice(bits * width, (bits + 1) * width)
-        parts(rhs_here, slice(0, depth), slice(at, at + width), out_high, out_low, columns)
+        parts(rhs, slice(0, depth), pl.ds(pl.multiple_of(place, width), width), out_high, out_low, columns)
 
     def multiply(number):
         _, bits, out, out_high, out_low = blocks[number]
@@ -144,8 +134,6 @@
         both = dot(projected[...], out_high[:, columns])
         out[:, columns] = both[:rank] + both[rank:] + dot(projected[:rank], out_low[:, columns])
 
-    for number in range(2):
-        rhs_copies[number].wait()
     for low_column in range(0, depth, width):
         columns = slice(low_column, low_column + width)
         both = dot(turned[...], inverse_high[:, columns])
@@ -156,30 +144,18 @@
     prepare(1)
     for number in range(0, len(blocks), 2):
         later = range(number + 2, min(number + 4, len(blocks)))
-        for other in later:
-            rhs_copies[other].wait()
         multiply(number)
         multiply(number + 1)
         for other in later:
             prepare(other)
-    for copy in matrix_copies:
-        copy.wait()
-
-    @pl.when(core == 0)
-    def _():
-        mixed[...] = joined[...]
-
-    @pl.when(core != 0)
-    def _():
-        mixed[: packed.shape[0]] = packed[...]
-        mixed[packed.shape[0] :] = jnp.zeros_like(mixed[packed.shape[0] :])
 
 
 def leaf_body(add, inverse_high, inverse_low, rhs_high, rhs_low, *rest):
     out = rest[-1]
-    tile = out.shape[0] // 4
-
-    @pl.loop(0, 4)
+    tiles = 2
+    tile = out.shape[0] // tiles
+
+    @pl.loop(0, tiles)
     def _(step):
         rows = pl.ds(pl.multiple_of(step * tile, tile), tile)
         left_high, left_low = inverse_high[rows], inverse_low[rows]
@@ -374,9 +350,11 @@
         high, low = split(uppers[bits][...])
         for part, value in enumerate((high, high, low)):
             stack[pl.ds(pl.multiple_of(part * couple + place * rank, rank), rank)] = value
-    for bits in range(arity):
-        rows = slice(bits * rank, (bits + 1) * rank)
-        outs[bits][...] = solve[rows] - dot(down_map[rows], stack[...])
+    for bits in range(0, arity, 2):
+        rows = slice(bits * rank, (bits + 2) * rank)
+        down = solve[rows] - dot(down_map[rows], stack[...])
+        outs[bits][...] = down[:rank]
+        outs[bits + 1][...] = down[rank:]
 
 
 def stack_second_body(arity, ids, node_slots, *refs):
@@ -494,38 +472,48 @@
     ids = jnp.stack([position, core]).astype(jnp.int32)
 
     vmem = pl.BlockSpec(memory_space=pltpu.VMEM)
-    large = [leaf_basis, leaf_inverse, rhs_block, couple_one, basis_one, couple_two, basis_two, root_inverse]
+    hbm = pl.BlockSpec(memory_space=pl.ANY)
+
+    def in_hbm(arrays):
+        return [pltpu.with_memory_space_constraint(array, pltpu.HBM) for array in arrays]
+
+    matrices = [couple_one, basis_one, couple_two, basis_two, root_inverse]
+    pack = pl.pallas_call(
+        pack_body,
+        out_shape=[struct(rank, joined_width), struct(packed_rows, joined_width), struct(rank, joined_width)],
+        in_specs=[pl.BlockSpec(memory_space=pltpu.SMEM)] + [hbm] * len(matrices),
+        out_specs=[vmem] * 3,
+        scratch_shapes=[pltpu.SemaphoreType.DMA((4 + wide // min(wide, couple),))],
+        compiler_params=pltpu.CompilerParams(vmem_limit_bytes=16 << 20),
+        cost_estimate=pl.CostEstimate(flops=20_000_000_000, bytes_accessed=20 << 20, transcendentals=0),
+    )
+    joined_mine, packed, mixed_mine = pack(ids, *in_hbm(matrices))
+    one = swap_each(mixed_mine, (1, arity))
+    two = swap_each(joined_mine, (2, 3))
+    three = swap_each(packed, (2 * arity, 3 * arity))
+
+    large = [leaf_basis, leaf_inverse, rhs_block]
     coeff = pl.pallas_call(
         functools.partial(coeff_body, arity),
         out_shape=[struct(rank, half)] * 2
         + [struct(points, 3 * rank, dtype=BF16)]
         + [struct(points, depth, dtype=BF16)] * 2
-        + [struct(depth, half, dtype=BF16)] * 4
-        + [struct(rank, joined_width), struct(packed_rows, joined_width), struct(rank, joined_width)],
-        in_specs=[pl.BlockSpec(memory_space=pltpu.SMEM)] + [pl.BlockSpec(memory_space=pl.ANY)] * len(large),
-        out_specs=[vmem] * 12,
+        + [struct(depth, half, dtype=BF16)] * 4,
+        in_specs=[pl.BlockSpec(memory_space=pltpu.SMEM)] + [vmem] * len(large),
+        out_specs=[vmem] * 9,
         scratch_shapes=[
-            pltpu.VMEM((points, rank), F32),
-            pltpu.VMEM((points, depth), F32),
-            pltpu.VMEM((depth, 2 * half), F32),
             pltpu.VMEM((2 * rank, points), BF16),
             pltpu.VMEM((2 * rank, depth), BF16),
-            pltpu.SemaphoreType.DMA((5 + 3 * arity + wide // min(wide, couple),)),
         ],
         compiler_params=pltpu.CompilerParams(vmem_limit_bytes=16 << 20),
         cost_estimate=pl.CostEstimate(
             flops=6 * rank * depth * (points + 2 * half), bytes_accessed=14 << 20, transcendentals=0
         ),
     )
-    coeff_send, coeff_own, basis_parts, *halves, joined_mine, packed, mixed_mine = coeff(
-        ids, *[pltpu.with_memory_space_constraint(array, pltpu.HBM) for array in large]
-    )
+    coeff_send, coeff_own, basis_parts, *halves = coeff(ids, *large)
     inverse_parts, rhs_other, rhs_own = halves[:2], halves[2:4], halves[4:]
     coeff_got = swap_core(coeff_send)
 
-    one = swap_each(mixed_mine, (1, arity))
-    two = swap_each(joined_mine, (2, 3))
-    three = swap_each(packed, (2 * arity, 3 * arity))
     one_other = swap_core(one)
     two_other = swap_core(two)
     three_other = swap_core(three)

time: 77.9 us -> 81.7 us (1.049)
  local copies, waits for them, and re-layouts: 0.01 us -> 4.83 us
  Pallas kernels: 24.6 us -> 23.2 us
    unnamed x4 -> x10, local copies, waits for them, and re-layouts: 0.01 us -> 4.83 us
    pallas_call x1 -> x2, Pallas kernels: 5.22 us -> 4.41 us  [the longest x1 2.84 us: per_device(): coeff_send, coeff_own, basis_parts, *halves = coeff(ids, *large)]
where the time goes in v2:
time: 81.7 us; the launch traced here: 81.5 us
  waiting for transfers between devices  28.5 us (35%)
  starting transfers between devices  24.7 us (30%)
  Pallas kernels  23.2 us (28%)
  local copies, waits for them, and re-layouts  4.83 us (6%)
    ppermute x10, waiting for transfers between devices, swap(): lax.ppermute(block, 'leaf', [(low, low ^ bits) for low in range(count)])  15.9 us
    pallas_call x9, Pallas kernels, call(): pl.pallas_call(body, out_shape=out_shapes, in_specs=[pl.BlockSpec(memory_...  14.3 us
    ppermute x10, starting transfers between devices, swap(): lax.ppermute(block, 'leaf', [(low, low ^ bits) for low in range(count)])  13.6 us
    ppermute x4, waiting for transfers between devices, swap_each(): return lax.ppermute(block, ('leaf', 'rhs'), route)  11.3 us
    ppermute x4, starting transfers between devices, swap_each(): return lax.ppermute(block, ('leaf', 'rhs'), route)  8.73 us
    unnamed x10, local copies, waits for them, and re-layouts  4.83 us
    pallas_call x2, Pallas kernels, final(): pl.pallas_call(functools.partial(final_body, first, half // width), out_s...  4.43 us
    pallas_call x1, Pallas kernels, per_device(): coeff_send, coeff_own, basis_parts, *halves = coeff(ids, *large)  2.84 us
  transfers between devices with their start and end apart: 21, of which 11 were waited for; matrix products, arithmetic and copies ran while one was open for 0% of the time, Pallas kernels for 17%

profile of v2, /device:TPU:0, one launch (start us, length us, event | category | flops | bytes accessed | tf_op | source)
XLA Modules:
  0.0 81.5 jit_solution(13373382140693185462)
XLA Ops:
  0.0 0.1 pad_add_fusion.ids
  0.1 0.0 copy-start
  0.1 2.2 %copy-done = f32[512,2048]{1,0:T(8,128)S(1)} copy-done((f32[512,2048]{1,0:T(8,128)S(1)}, f32[512,2048]{1,0:T(8,128)}, u32[]{:S(2)}) %copy-start) | copy-done | bytes 4194328
  2.3 1.6 %copy-done.1 = f32[1024,512]{1,0:T(8,128)S(1)} copy-done((f32[1024,512]{1,0:T(8,128)S(1)}, f32[1024,512]{1,0:T(8,128)}, u32[]{:S(2)}) %copy-start.1) | copy-done | bytes 2097176
  3.9 1.0 %copy-done.2 = f32[1024,128]{1,0:T(8,128)S(1)} copy-done((f32[1024,128]{1,0:T(8,128)S(1)}, f32[1024,128]{1,0:T(8,128)}, u32[]{:S(2)}) %copy-start.2) | copy-done | bytes 524312
  4.9 2.8 %shard_map.100 = (f32[128,1024]{1,0:T(8,128)S(1)}, f32[128,1024]{1,0:T(8,128)S(1)}, bf16[1024,384]{1,0:T(8,128)(2,1)S(1)}, bf16[1024,512]{1,0:T(8,128)(2,1)S(1)}...) custom-call(s32[2]{0:T(128)S(1)} %pad_add_fusion.ids, ...), custom_call_target="tpu_custom_call" | custom-call | flops 1207959552 | bytes 14680064 | tf_op jit(solution)/shard_map/pallas_call | solution.py:513
  7.7 3.6 %shard_map.101 = f32[1024,1024]{1,0:T(8,128)S(1)} custom-call(bf16[1024,512]{1,0:T(8,128)(2,1)S(1)} %get-tuple-element.33.inverse_high, bf16[1024,512]{1,0:T(8,128)(2,1)S(1)} %get-tuple-element.34.inverse_low, bf16[512,1024]{1,0:T(8,128)(2,1)S(1)} %get-tuple-element.37.rhs_high, bf16[512,1024]{1,0:T(8,128)(2,1)S(1)} %get-tuple-element.38.rhs_low), custom_call_target="tpu_custom_call" | custom-call | flops 3221225472 | bytes 8388608 | tf_op jit(solution)/shard_map/pallas_call | solution.py:37
  11.3 0.0 copy-start.4
  11.3 0.6 collective-permute-start
  11.9 1.6 %shard_map.103 = (f32[128,640]{1,0:T(8,128)S(1)}, f32[40,640]{1,0:T(8,128)S(1)}, f32[128,640]{1,0:T(8,128)S(1)}) custom-call(s32[2]{0:T(128)S(1)} %pad_add_fusion.ids, f32[128,512]{1,0:T(8,128)} %couple_one.1, f32[128,128]{1,0:T(8,128)} %basis_one.1, f32[32,512]{1,0:T(8,128)} %couple_two.1, f32[32,128]{1,0:T(8,128)} %basis_two.1, f32[8,128]{1,0:T(8,128)} %root.1), custom_call_target="tpu_custom_call" | custom-call | flops 20000000000 | bytes 20971520 | tf_op jit(solution)/shard_map/pallas_call | solution.py:490
  13.5 0.0 copy-start.3
  13.5 2.6 %collective-permute-start.1 = (f32[128,640]{1,0:T(8,128)S(1)}, f32[128,640]{1,0:T(8,128)S(1)}, u32[]{:S(2)}, u32[]{:S(2)}) collective-permute-start(f32[128,640]{1,0:T(8,128)S(1)} %get-tuple-element.41), channel_id=1, source_target_pairs={{0,2},{1,9},{2,0},{3,11},{4,6},{5,13},{6,4},{7,15},{8,10},{9,1},{1... | collective-permute-start | bytes 983048 | tf_op jit(solution)/shard_map/ppermute | solution.py:442
  16.0 5.1 %collective-permute-done.1.one = f32[128,640]{1,0:T(8,128)S(1)} collective-permute-done((f32[128,640]{1,0:T(8,128)S(1)}, f32[128,640]{1,0:T(8,128)S(1)}, u32[]{:S(2)}, u32[]{:S(2)}) %collective-permute-start.1) | collective-permute-done | bytes 327712 | tf_op jit(solution)/shard_map/ppermute | solution.py:442
  21.1 0.0 collective-permute-start.2
  21.1 3.1 %collective-permute-start.3 = (f32[40,640]{1,0:T(8,128)S(1)}, f32[40,640]{1,0:T(8,128)S(1)}, u32[]{:S(2)}, u32[]{:S(2)}) collective-permute-start(f32[40,640]{1,0:T(8,128)S(1)} %get-tuple-element.40.packed), channel_id=1, source_target_pairs={{0,16},{1,25},{2,18},{3,27},{4,20},{5,29},{6,22},{7,31},{8,24},{9,... | collective-permute-start | bytes 307208 | tf_op jit(solution)/shard_map/ppermute | solution.py:442
  24.2 1.5 %collective-permute-start.9 = (f32[128,640]{1,0:T(8,128)S(1)}, f32[128,640]{1,0:T(8,128)S(1)}, u32[]{:S(2)}, u32[]{:S(2)}) collective-permute-start(f32[128,640]{1,0:T(8,128)S(1)} %get-tuple-element.44.mine), channel_id=1, source_target_pairs={{0,4},{1,7},{2,6},{3,5},{4,0},{5,3},{6,2},{7,1},{8,12},{9,15},{10,... | collective-permute-start | bytes 983048 | tf_op jit(solution)/shard_map/ppermute | solution.py:442
  25.7 1.9 %collective-permute-start.11 = (f32[128,1024]{1,0:T(8,128)S(1)}, f32[128,1024]{1,0:T(8,128)S(1)}, u32[]{:S(2)}, u32[]{:S(2)}) collective-permute-start(f32[128,1024]{1,0:T(8,128)S(1)} %get-tuple-element.48), channel_id=1, source_target_pairs={{0,1},{1,0},{2,3},{3,2},{4,5},{5,4},{6,7},{7,6},{8,9},{9,8},{10,11... | collective-permute-start | bytes 1572872 | tf_op jit(solution)/shard_map/ppermute | solution.py:431
  27.6 2.5 %collective-permute-done.3.three = f32[40,640]{1,0:T(8,128)S(1)} collective-permute-done((f32[40,640]{1,0:T(8,128)S(1)}, f32[40,640]{1,0:T(8,128)S(1)}, u32[]{:S(2)}, u32[]{:S(2)}) %collective-permute-start.3) | collective-permute-done | bytes 102432 | tf_op jit(solution)/shard_map/ppermute | solution.py:442
  30.1 0.0 collective-permute-start.4
  30.1 1.3 %collective-permute-done.4.three_other = f32[40,640]{1,0:T(8,128)S(1)} collective-permute-done((f32[40,640]{1,0:T(8,128)S(1)}, f32[40,640]{1,0:T(8,128)S(1)}, u32[]{:S(2)}, u32[]{:S(2)}) %collective-permute-start.4) | collective-permute-done | bytes 102432 | tf_op jit(solution)/shard_map/ppermute | solution.py:431
  31.4 0.0 collective-permute-done.2.one_other
  31.4 0.6 shard_map.104
  32.1 1.5 %collective-permute-start.5 = (f32[144,640]{1,0:T(8,128)S(1)}, f32[144,640]{1,0:T(8,128)S(1)}, u32[]{:S(2)}, u32[]{:S(2)}) collective-permute-start(f32[144,640]{1,0:T(8,128)S(1)} %get-tuple-element.42.mine), channel_id=1, source_target_pairs={{0,2},{1,5},{2,0},{3,7},{4,6},{5,1},{6,4},{7,3},{8,10},{9,13},{10,... | collective-permute-start | bytes 1105928 | tf_op jit(solution)/shard_map/ppermute | solution.py:442
  33.6 1.2 %collective-permute-done.9.two = f32[128,640]{1,0:T(8,128)S(1)} collective-permute-done((f32[128,640]{1,0:T(8,128)S(1)}, f32[128,640]{1,0:T(8,128)S(1)}, u32[]{:S(2)}, u32[]{:S(2)}) %collective-permute-start.9) | collective-permute-done | bytes 327712 | tf_op jit(solution)/shard_map/ppermute | solution.py:442
  34.8 0.0 collective-permute-start.10
  34.8 2.4 %collective-permute-start.7 = (f32[72,640]{1,0:T(8,128)S(1)}, f32[72,640]{1,0:T(8,128)S(1)}, u32[]{:S(2)}, u32[]{:S(2)}) collective-permute-start(f32[72,640]{1,0:T(8,128)S(1)} %get-tuple-element.43), channel_id=1, source_target_pairs={{0,6},{2,4},{4,2},{6,0},{8,14},{10,12},{12,10},{14,8},{16,22},{18,... | collective-permute-start | bytes 552968 | tf_op jit(solution)/shard_map/ppermute | solution.py:427
  37.2 0.0 collective-permute-done.11.got
  37.2 0.1 shard_map.106
  37.3 0.6 collective-permute-start.12
  37.9 2.5 %collective-permute-done.5.near = f32[144,640]{1,0:T(8,128)S(1)} collective-permute-done((f32[144,640]{1,0:T(8,128)S(1)}, f32[144,640]{1,0:T(8,128)S(1)}, u32[]{:S(2)}, u32[]{:S(2)}) %collective-permute-start.5) | collective-permute-done | bytes 368672 | tf_op jit(solution)/shard_map/ppermute | solution.py:442
  40.4 0.0 collective-permute-start.6
  40.4 5.5 %collective-permute-done.7.far = f32[72,640]{1,0:T(8,128)S(1)} collective-permute-done((f32[72,640]{1,0:T(8,128)S(1)}, f32[72,640]{1,0:T(8,128)S(1)}, u32[]{:S(2)}, u32[]{:S(2)}) %collective-permute-start.7) | collective-permute-done | bytes 184352 | tf_op jit(solution)/shard_map/ppermute | solution.py:427
  46.0 0.0 collective-permute-start.8
  46.0 0.0 collective-permute-done.10.two_other
  46.0 0.0 collective-permute-start.13
  46.0 0.4 collective-permute-done.12.refs_1_
  46.4 2.5 %collective-permute-start.14 = (f32[128,256]{1,0:T(8,128)S(1)}, f32[128,256]{1,0:T(8,128)S(1)}, u32[]{:S(2)}, u32[]{:S(2)}) collective-permute-start(f32[128,256]{1,0:T(8,128)S(1)} %get-tuple-element.52), channel_id=1, source_target_pairs={{0,6},{2,4},{4,2},{6,0},{8,14},{10,12},{12,10},{14,8},{16,22},{18,... | collective-permute-start | bytes 393224 | tf_op jit(solution)/shard_map/ppermute | solution.py:427
  48.9 1.1 %shard_map.105 = (f32[4,128,640]{2,1,0:T(8,128)S(1)}, bf16[128,1536]{1,0:T(8,128)(2,1)S(1)}) custom-call(s32[2]{0:T(128)S(1)} %pad_add_fusion.ids, f32[128,640]{1,0:T(8,128)S(1)} %get-tuple-element.44.mine, f32[128,640]{1,0:T(8,128)S(1)} %collective-permute-done.1.one, f32[128,640]{1,0:T(8,128)S(1)} %collective-permute-done.2.one_other, ...), custom_call_target="tpu_custom_call" | custom-call | flops 201326592 | bytes 3342336 | tf_op jit(solution)/shard_map/pallas_call | solution.py:37
  50.0 4.7 %collective-permute-done.13.refs_2_ = f32[128,256]{1,0:T(8,128)S(1)} collective-permute-done((f32[128,256]{1,0:T(8,128)S(1)}, f32[128,256]{1,0:T(8,128)S(1)}, u32[]{:S(2)}, u32[]{:S(2)}) %collective-permute-start.13) | collective-permute-done | bytes 131104 | tf_op jit(solution)/shard_map/ppermute | solution.py:427
  54.7 0.0 collective-permute-done.14.refs_3_
  54.7 0.0 copy-done.4
  54.7 0.9 %shard_map.107 = (f32[128,256]{1,0:T(8,128)S(1)}, bf16[1536,256]{1,0:T(8,128)(2,1)S(1)}) custom-call(s32[2]{0:T(128)S(1)} %pad_add_fusion.ids, s32[16]{0:T(128)S(1)} %copy-done.4, bf16[128,1536]{1,0:T(8,128)(2,1)S(1)} %get-tuple-element.46.reduced, f32[128,256]{1,0:T(8,128)S(1)} %get-tuple-element.49.refs_0_, ...), custom_call_target="tpu_custom_call" | custom-call | flops 100663296 | bytes 1835008 | tf_op jit(solution)/shard_map/pallas_call | solution.py:37
  55.6 2.8 %collective-permute-start.17 = (f32[128,256]{1,0:T(8,128)S(1)}, f32[128,256]{1,0:T(8,128)S(1)}, u32[]{:S(2)}, u32[]{:S(2)}) collective-permute-start(f32[128,256]{1,0:T(8,128)S(1)} %get-tuple-element.56.refs_0_), channel_id=1, source_target_pairs={{0,24},{2,26},{4,28},{6,30},{8,16},{10,18},{12,20},{14,22},{16,8},... | collective-permute-start | bytes 393224 | tf_op jit(solution)/shard_map/ppermute | solution.py:427
  58.4 0.0 collective-permute-start.16
  58.4 0.0 collective-permute-done.8.far_other
  58.4 1.6 %collective-permute-start.15 = (f32[128,256]{1,0:T(8,128)S(1)}, f32[128,256]{1,0:T(8,128)S(1)}, u32[]{:S(2)}, u32[]{:S(2)}) collective-permute-start(f32[128,256]{1,0:T(8,128)S(1)} %get-tuple-element.56.refs_0_), channel_id=1, source_target_pairs={{0,8},{2,10},{4,12},{6,14},{8,0},{10,2},{12,4},{14,6},{16,24},{18,... | collective-permute-start | bytes 393224 | tf_op jit(solution)/shard_map/ppermute | solution.py:427
  60.1 1.1 %shard_map.108 = (f32[512,256]{1,0:T(8,128)S(1)}, f32[512,128]{1,0:T(8,128)S(1)}) custom-call(s32[2]{0:T(128)S(1)} %pad_add_fusion.ids, s32[16]{0:T(128)S(1)} %copy-done.4, f32[4,128,640]{2,1,0:T(8,128)S(1)} %get-tuple-element.45.joined, bf16[1536,256]{1,0:T(8,128)(2,1)S(1)} %get-tuple-element.53.stack), custom_call_target="tpu_custom_call" | custom-call | flops 402653184 | bytes 2883584 | tf_op jit(solution)/shard_map/pallas_call | solution.py:37
  61.2 0.0 collective-permute-done.6.near_other
  61.2 0.0 copy-done.3
  61.2 2.1 %shard_map.109.down_map = bf16[512,1536]{1,0:T(8,128)(2,1)S(1)} custom-call(s32[2]{0:T(128)S(1)} %pad_add_fusion.ids, s32[4]{0:T(128)S(1)} %copy-done.3, f32[144,640]{1,0:T(8,128)S(1)} %get-tuple-element.42.mine, f32[144,640]{1,0:T(8,128)S(1)} %collective-permute-done.5.near, f32[144,640]{1,0:T(8,128)S(1)} %collective-permute-done.6.near_other, ...), custom_call_target="tpu_custom_call" | custom-call | flops 201326592 | bytes 3309568 | tf_op jit(solution)/shard_map/pallas_call | solution.py:37
  63.4 0.6 collective-permute-done.17.refs_3_
  63.9 4.2 %collective-permute-done.16.refs_2_ = f32[128,256]{1,0:T(8,128)S(1)} collective-permute-done((f32[128,256]{1,0:T(8,128)S(1)}, f32[128,256]{1,0:T(8,128)S(1)}, u32[]{:S(2)}, u32[]{:S(2)}) %collective-permute-start.16) | collective-permute-done | bytes 131104 | tf_op jit(solution)/shard_map/ppermute | solution.py:427
  68.1 0.0 collective-permute-done.15.refs_1_
  68.1 1.2 %shard_map.110 = (f32[128,256]{1,0:T(8,128)S(1)}, f32[128,256]{1,0:T(8,128)S(1)}, f32[128,256]{1,0:T(8,128)S(1)}, f32[128,256]{1,0:T(8,128)S(1)}) custom-call(s32[2]{0:T(128)S(1)} %pad_add_fusion.ids, s32[4]{0:T(128)S(1)} %copy-done.3, bf16[512,1536]{1,0:T(8,128)(2,1)S(1)} %shard_map.109.down_map, f32[512,256]{1,0:T(8,128)S(1)} %get-tuple-element.55.solve, ...), custom_call_target="tpu_custom_call" | custom-call | flops 402653184 | bytes 3145728 | tf_op jit(solution)/shard_map/pallas_call | solution.py:37
  69.4 1.5 %collective-permute-start.18 = (f32[128,256]{1,0:T(8,128)S(1)}, f32[128,256]{1,0:T(8,128)S(1)}, u32[]{:S(2)}, u32[]{:S(2)}) collective-permute-start(f32[128,256]{1,0:T(8,128)S(1)} %get-tuple-element.57), channel_id=1, source_target_pairs={{0,2},{2,0},{4,6},{6,4},{8,10},{10,8},{12,14},{14,12},{16,18},{18,... | collective-permute-start | bytes 393224 | tf_op jit(solution)/shard_map/ppermute | solution.py:427
  70.9 0.6 collective-permute-start.19
  71.5 1.4 %collective-permute-start.20 = (f32[128,256]{1,0:T(8,128)S(1)}, f32[128,256]{1,0:T(8,128)S(1)}, u32[]{:S(2)}, u32[]{:S(2)}) collective-permute-start(f32[128,256]{1,0:T(8,128)S(1)} %get-tuple-element.59), channel_id=1, source_target_pairs={{0,6},{2,4},{4,2},{6,0},{8,14},{10,12},{12,10},{14,8},{16,22},{18,... | collective-permute-start | bytes 393224 | tf_op jit(solution)/shard_map/ppermute | solution.py:427
  72.9 0.0 collective-permute-done.rest_0_
  72.9 3.6 %shard_map.102.base = f32[1024,1024]{1,0:T(8,128)S(1)} custom-call(bf16[1024,512]{1,0:T(8,128)(2,1)S(1)} %get-tuple-element.33.inverse_high, bf16[1024,512]{1,0:T(8,128)(2,1)S(1)} %get-tuple-element.34.inverse_low, bf16[512,1024]{1,0:T(8,128)(2,1)S(1)} %get-tuple-element.35.rhs_high, bf16[512,1024]{1,0:T(8,128)(2,1)S(1)} %get-tuple-element.36.rhs_low, ...), custom_call_target="tpu_custom_call" | custom-call | flops 3221225472 | bytes 12582912 | tf_op jit(solution)/shard_map/pallas_call | solution.py:37
  76.5 1.8 %shard_map.111.refs_3_ = f32[1024,1024]{1,0:T(8,128)} custom-call(s32[2]{0:T(128)S(1)} %pad_add_fusion.ids, f32[1024,1024]{1,0:T(8,128)S(1)} %shard_map.102.base, bf16[1024,384]{1,0:T(8,128)(2,1)S(1)} %get-tuple-element.39.left, f32[128,256]{1,0:T(8,128)S(1)} %get-tuple-element.60.refs_0_), custom_call_target="tpu_custom_call" | custom-call | flops 201326592 | bytes 2097152 | tf_op jit(solution)/shard_map/pallas_call | solution.py:405
  78.4 0.0 collective-permute-done.18.refs_0_
  78.4 0.5 collective-permute-done.19.refs_1_
  78.9 0.0 collective-permute-done.20.refs_2_
  78.9 2.6 %shard_map.112 = f32[1024,1024]{1,0:T(8,128)} custom-call(s32[2]{0:T(128)S(1)} %pad_add_fusion.ids, f32[1024,1024]{1,0:T(8,128)S(1)} %shard_map.102.base, bf16[1024,384]{1,0:T(8,128)(2,1)S(1)} %get-tuple-element.39.left, f32[128,256]{1,0:T(8,128)S(1)} %collective-permute-done.18.refs_0_, ...), custom_call_target="tpu_custom_call", output_to_operand_aliasing={{}: (6, {})} | custom-call | flops 603979776 | bytes 6291456 | tf_op jit(solution)/shard_map/pallas_call | solution.py:405
  (2 shorter events, 0.0 us)
Async XLA Ops:
  0.1 2.2 %copy-start = (f32[512,2048]{1,0:T(8,128)S(1)}, f32[512,2048]{1,0:T(8,128)}, u32[]{:S(2)}) copy-start(f32[512,2048]{1,0:T(8,128)} %rhs.1) | copy-start | bytes 12582916
  2.3 1.6 %copy-start.1 = (f32[1024,512]{1,0:T(8,128)S(1)}, f32[1024,512]{1,0:T(8,128)}, u32[]{:S(2)}) copy-start(f32[1024,512]{1,0:T(8,128)} %inverse.1) | copy-start | bytes 6291460
  3.9 1.0 %copy-start.2 = (f32[1024,128]{1,0:T(8,128)S(1)}, f32[1024,128]{1,0:T(8,128)}, u32[]{:S(2)}) copy-start(f32[1024,128]{1,0:T(8,128)} %basis.1) | copy-start | bytes 1572868
  11.3 43.4 %copy-start.4 = (s32[16]{0:T(128)S(1)}, s32[16]{0:T(128)}, u32[]{:S(2)}) copy-start(s32[16]{0:T(128)} %slots.3) | copy-start | bytes 196
  11.3 61.6 %collective-permute-start = (f32[1024,1024]{1,0:T(8,128)S(1)}, f32[1024,1024]{1,0:T(8,128)S(1)}, u32[]{:S(2)}, u32[]{:S(2)}) collective-permute-start(f32[1024,1024]{1,0:T(8,128)S(1)} %shard_map.101), channel_id=1, source_target_pairs={{0,1},{1,0},{2,3},{3,2},{4,5},{5,4},{6,7},{7,6},{8,9},{9,8},{10,11... | collective-permute-start | bytes 12582920 | tf_op jit(solution)/shard_map/ppermute | solution.py:431
  13.5 47.7 %copy-start.3 = (s32[4]{0:T(128)S(1)}, s32[4]{0:T(128)}, u32[]{:S(2)}) copy-start(s32[4]{0:T(128)} %node_slots.3) | copy-start | bytes 52
  13.5 7.6 %collective-permute-start.1 = (f32[128,640]{1,0:T(8,128)S(1)}, f32[128,640]{1,0:T(8,128)S(1)}, u32[]{:S(2)}, u32[]{:S(2)}) collective-permute-start(f32[128,640]{1,0:T(8,128)S(1)} %get-tuple-element.41), channel_id=1, source_target_pairs={{0,2},{1,9},{2,0},{3,11},{4,6},{5,13},{6,4},{7,15},{8,10},{9,1},{1... | collective-permute-start | bytes 983048 | tf_op jit(solution)/shard_map/ppermute | solution.py:442
  21.1 10.4 %collective-permute-start.2 = (f32[128,640]{1,0:T(8,128)S(1)}, f32[128,640]{1,0:T(8,128)S(1)}, u32[]{:S(2)}, u32[]{:S(2)}) collective-permute-start(f32[128,640]{1,0:T(8,128)S(1)} %collective-permute-done.1.one), channel_id=1, source_target_pairs={{0,1},{1,0},{2,3},{3,2},{4,5},{5,4},{6,7},{7,6},{8,9},{9,8},{10,11... | collective-permute-start | bytes 983048 | tf_op jit(solution)/shard_map/ppermute | solution.py:431
  21.1 9.0 %collective-permute-start.3 = (f32[40,640]{1,0:T(8,128)S(1)}, f32[40,640]{1,0:T(8,128)S(1)}, u32[]{:S(2)}, u32[]{:S(2)}) collective-permute-start(f32[40,640]{1,0:T(8,128)S(1)} %get-tuple-element.40.packed), channel_id=1, source_target_pairs={{0,16},{1,25},{2,18},{3,27},{4,20},{5,29},{6,22},{7,31},{8,24},{9,... | collective-permute-start | bytes 307208 | tf_op jit(solution)/shard_map/ppermute | solution.py:442
  24.2 10.6 %collective-permute-start.9 = (f32[128,640]{1,0:T(8,128)S(1)}, f32[128,640]{1,0:T(8,128)S(1)}, u32[]{:S(2)}, u32[]{:S(2)}) collective-permute-start(f32[128,640]{1,0:T(8,128)S(1)} %get-tuple-element.44.mine), channel_id=1, source_target_pairs={{0,4},{1,7},{2,6},{3,5},{4,0},{5,3},{6,2},{7,1},{8,12},{9,15},{10,... | collective-permute-start | bytes 983048 | tf_op jit(solution)/shard_map/ppermute | solution.py:442
  25.7 11.5 %collective-permute-start.11 = (f32[128,1024]{1,0:T(8,128)S(1)}, f32[128,1024]{1,0:T(8,128)S(1)}, u32[]{:S(2)}, u32[]{:S(2)}) collective-permute-start(f32[128,1024]{1,0:T(8,128)S(1)} %get-tuple-element.48), channel_id=1, source_target_pairs={{0,1},{1,0},{2,3},{3,2},{4,5},{5,4},{6,7},{7,6},{8,9},{9,8},{10,11... | collective-permute-start | bytes 1572872 | tf_op jit(solution)/shard_map/ppermute | solution.py:431
  30.1 1.3 %collective-permute-start.4 = (f32[40,640]{1,0:T(8,128)S(1)}, f32[40,640]{1,0:T(8,128)S(1)}, u32[]{:S(2)}, u32[]{:S(2)}) collective-permute-start(f32[40,640]{1,0:T(8,128)S(1)} %collective-permute-done.3.three), channel_id=1, source_target_pairs={{0,1},{1,0},{2,3},{3,2},{4,5},{5,4},{6,7},{7,6},{8,9},{9,8},{10,11... | collective-permute-start | bytes 307208 | tf_op jit(solution)/shard_map/ppermute | solution.py:431
  32.1 8.4 %collective-permute-start.5 = (f32[144,640]{1,0:T(8,128)S(1)}, f32[144,640]{1,0:T(8,128)S(1)}, u32[]{:S(2)}, u32[]{:S(2)}) collective-permute-start(f32[144,640]{1,0:T(8,128)S(1)} %get-tuple-element.42.mine), channel_id=1, source_target_pairs={{0,2},{1,5},{2,0},{3,7},{4,6},{5,1},{6,4},{7,3},{8,10},{9,13},{10,... | collective-permute-start | bytes 1105928 | tf_op jit(solution)/shard_map/ppermute | solution.py:442
  34.8 11.1 %collective-permute-start.10 = (f32[128,640]{1,0:T(8,128)S(1)}, f32[128,640]{1,0:T(8,128)S(1)}, u32[]{:S(2)}, u32[]{:S(2)}) collective-permute-start(f32[128,640]{1,0:T(8,128)S(1)} %collective-permute-done.9.two), channel_id=1, source_target_pairs={{0,1},{1,0},{2,3},{3,2},{4,5},{5,4},{6,7},{7,6},{8,9},{9,8},{10,11... | collective-permute-start | bytes 983048 | tf_op jit(solution)/shard_map/ppermute | solution.py:431
  34.8 11.1 %collective-permute-start.7 = (f32[72,640]{1,0:T(8,128)S(1)}, f32[72,640]{1,0:T(8,128)S(1)}, u32[]{:S(2)}, u32[]{:S(2)}) collective-permute-start(f32[72,640]{1,0:T(8,128)S(1)} %get-tuple-element.43), channel_id=1, source_target_pairs={{0,6},{2,4},{4,2},{6,0},{8,14},{10,12},{12,10},{14,8},{16,22},{18,... | collective-permute-start | bytes 552968 | tf_op jit(solution)/shard_map/ppermute | solution.py:427
  37.3 9.1 %collective-permute-start.12 = (f32[128,256]{1,0:T(8,128)S(1)}, f32[128,256]{1,0:T(8,128)S(1)}, u32[]{:S(2)}, u32[]{:S(2)}) collective-permute-start(f32[128,256]{1,0:T(8,128)S(1)} %get-tuple-element.50), channel_id=1, source_target_pairs={{0,2},{2,0},{4,6},{6,4},{8,10},{10,8},{12,14},{14,12},{16,18},{18,... | collective-permute-start | bytes 393224 | tf_op jit(solution)/shard_map/ppermute | solution.py:427
  40.4 20.8 %collective-permute-start.6 = (f32[144,640]{1,0:T(8,128)S(1)}, f32[144,640]{1,0:T(8,128)S(1)}, u32[]{:S(2)}, u32[]{:S(2)}) collective-permute-start(f32[144,640]{1,0:T(8,128)S(1)} %collective-permute-done.5.near), channel_id=1, source_target_pairs={{0,1},{1,0},{2,3},{3,2},{4,5},{5,4},{6,7},{7,6},{8,9},{9,8},{10,11... | collective-permute-start | bytes 1105928 | tf_op jit(solution)/shard_map/ppermute | solution.py:431
  46.0 12.5 %collective-permute-start.8 = (f32[72,640]{1,0:T(8,128)S(1)}, f32[72,640]{1,0:T(8,128)S(1)}, u32[]{:S(2)}, u32[]{:S(2)}) collective-permute-start(f32[72,640]{1,0:T(8,128)S(1)} %collective-permute-done.7.far), channel_id=1, source_target_pairs={{0,1},{1,0},{2,3},{3,2},{4,5},{5,4},{6,7},{7,6},{8,9},{9,8},{10,11... | collective-permute-start | bytes 552968 | tf_op jit(solution)/shard_map/ppermute | solution.py:431
  46.0 8.7 %collective-permute-start.13 = (f32[128,256]{1,0:T(8,128)S(1)}, f32[128,256]{1,0:T(8,128)S(1)}, u32[]{:S(2)}, u32[]{:S(2)}) collective-permute-start(f32[128,256]{1,0:T(8,128)S(1)} %get-tuple-element.51), channel_id=1, source_target_pairs={{0,4},{2,6},{4,0},{6,2},{8,12},{10,14},{12,8},{14,10},{16,20},{18,... | collective-permute-start | bytes 393224 | tf_op jit(solution)/shard_map/ppermute | solution.py:427
  46.4 8.3 %collective-permute-start.14 = (f32[128,256]{1,0:T(8,128)S(1)}, f32[128,256]{1,0:T(8,128)S(1)}, u32[]{:S(2)}, u32[]{:S(2)}) collective-permute-start(f32[128,256]{1,0:T(8,128)S(1)} %get-tuple-element.52), channel_id=1, source_target_pairs={{0,6},{2,4},{4,2},{6,0},{8,14},{10,12},{12,10},{14,8},{16,22},{18,... | collective-permute-start | bytes 393224 | tf_op jit(solution)/shard_map/ppermute | solution.py:427
  55.6 8.3 %collective-permute-start.17 = (f32[128,256]{1,0:T(8,128)S(1)}, f32[128,256]{1,0:T(8,128)S(1)}, u32[]{:S(2)}, u32[]{:S(2)}) collective-permute-start(f32[128,256]{1,0:T(8,128)S(1)} %get-tuple-element.56.refs_0_), channel_id=1, source_target_pairs={{0,24},{2,26},{4,28},{6,30},{8,16},{10,18},{12,20},{14,22},{16,8},... | collective-permute-start | bytes 393224 | tf_op jit(solution)/shard_map/ppermute | solution.py:427
  58.4 9.7 %collective-permute-start.16 = (f32[128,256]{1,0:T(8,128)S(1)}, f32[128,256]{1,0:T(8,128)S(1)}, u32[]{:S(2)}, u32[]{:S(2)}) collective-permute-start(f32[128,256]{1,0:T(8,128)S(1)} %get-tuple-element.56.refs_0_), channel_id=1, source_target_pairs={{0,16},{2,18},{4,20},{6,22},{8,24},{10,26},{12,28},{14,30},{16,0},... | collective-permute-start | bytes 393224 | tf_op jit(solution)/shard_map/ppermute | solution.py:427
  58.4 9.7 %collective-permute-start.15 = (f32[128,256]{1,0:T(8,128)S(1)}, f32[128,256]{1,0:T(8,128)S(1)}, u32[]{:S(2)}, u32[]{:S(2)}) collective-permute-start(f32[128,256]{1,0:T(8,128)S(1)} %get-tuple-element.56.refs_0_), channel_id=1, source_target_pairs={{0,8},{2,10},{4,12},{6,14},{8,0},{10,2},{12,4},{14,6},{16,24},{18,... | collective-permute-start | bytes 393224 | tf_op jit(solution)/shard_map/ppermute | solution.py:427
  69.4 9.0 %collective-permute-start.18 = (f32[128,256]{1,0:T(8,128)S(1)}, f32[128,256]{1,0:T(8,128)S(1)}, u32[]{:S(2)}, u32[]{:S(2)}) collective-permute-start(f32[128,256]{1,0:T(8,128)S(1)} %get-tuple-element.57), channel_id=1, source_target_pairs={{0,2},{2,0},{4,6},{6,4},{8,10},{10,8},{12,14},{14,12},{16,18},{18,... | collective-permute-start | bytes 393224 | tf_op jit(solution)/shard_map/ppermute | solution.py:427
  70.9 7.9 %collective-permute-start.19 = (f32[128,256]{1,0:T(8,128)S(1)}, f32[128,256]{1,0:T(8,128)S(1)}, u32[]{:S(2)}, u32[]{:S(2)}) collective-permute-start(f32[128,256]{1,0:T(8,128)S(1)} %get-tuple-element.58), channel_id=1, source_target_pairs={{0,4},{2,6},{4,0},{6,2},{8,12},{10,14},{12,8},{14,10},{16,20},{18,... | collective-permute-start | bytes 393224 | tf_op jit(solution)/shard_map/ppermute | solution.py:427
  71.5 7.4 %collective-permute-start.20 = (f32[128,256]{1,0:T(8,128)S(1)}, f32[128,256]{1,0:T(8,128)S(1)}, u32[]{:S(2)}, u32[]{:S(2)}) collective-permute-start(f32[128,256]{1,0:T(8,128)S(1)} %get-tuple-element.59), channel_id=1, source_target_pairs={{0,6},{2,4},{4,2},{6,0},{8,14},{10,12},{12,10},{14,8},{16,22},{18,... | collective-permute-start | bytes 393224 | tf_op jit(solution)/shard_map/ppermute | solution.py:427
